TPU v7x, 128 devices: a whole 4x4x4 slice. The times are simulated.
128 devices in a mesh: seq: 32 (over y, z, x_lo), head: 4 (over x_hi, core).
Axes of the slice: x: 4 (x_hi: 2, x_lo: 2; x = x_hi * 2 + x_lo), y: 4, z: 4, core: 2. Of those that a mesh axis runs over, the one named last changes fastest.
Arguments:
- query: bfloat16 [16384, 4096], P('seq', 'head'), may hold values from -46 to 46
- key_rows: bfloat16 [16384, 256], P('seq'), may hold values from -6 to 6
- value_rows: bfloat16 [16384, 256], P('seq'), may hold values from -6 to 6
- grad_out: bfloat16 [16384, 4096], P('seq', 'head'), may hold values from -6 to 6
Outputs:
- grad_query: bfloat16 [16384, 4096], P('seq', 'head')
- grad_key: float32 [16384, 256], P('seq')
- grad_value: float32 [16384, 256], P('seq')
All inputs are finite; a program needn't handle non-finite values.
Results may differ from a plain program's by a relative error of at most 0.0051.
Values may be sent and summed in bfloat16 or wider, within the bound.
A program may use at most 128 MiB of HBM per device.

v0:
```python
import jax
import jax.numpy as jnp
from jax import lax
from jax.sharding import PartitionSpec as P

WINDOW = 2048


def passed_along(block, axis, distance):
    devices = range(lax.axis_size(axis))
    route = [(i - distance, i) for i in devices if i - distance in devices]
    return lax.ppermute(block, axis, route)


def add_pair(first, second):
    return (first[0] + second[0], first[1] + second[1])


def return_halo(dk_ext, dv_ext, tok_rows, reach_shards):
    own_rows = (dk_ext[WINDOW:], dv_ext[WINDOW:])
    for distance in range(1, reach_shards + 1):
        lower = WINDOW - distance * tok_rows
        piece = (dk_ext[lower : lower + tok_rows], dv_ext[lower : lower + tok_rows])
        received = (
            passed_along(piece[0].astype(jnp.bfloat16), "seq", -distance).astype(jnp.float32),
            passed_along(piece[1].astype(jnp.bfloat16), "seq", -distance).astype(jnp.float32),
        )
        own_rows = add_pair(own_rows, received)
    return own_rows


def on_device(query, key_rows, value_rows, grad_out):
    tok_rows = key_rows.shape[0]
    head_dim = key_rows.shape[1]
    local_heads = query.shape[1] // head_dim
    reach_shards = WINDOW // tok_rows
    block_rows = min(512, tok_rows)
    score_scale = head_dim ** (-0.5)
    outgoing = (key_rows, value_rows)
    pieces = []
    for distance in range(reach_shards, 0, -1):
        pieces.append(passed_along((outgoing[0], outgoing[1]), "seq", distance))
    keys_halo = jnp.concatenate([piece[0] for piece in pieces], axis=0)
    values_halo = jnp.concatenate([piece[1] for piece in pieces], axis=0)
    keys_ext = jnp.concatenate([keys_halo, key_rows], axis=0)
    values_ext = jnp.concatenate([values_halo, value_rows], axis=0)
    offset = lax.axis_index("seq") * tok_rows
    row_ids = jnp.arange(block_rows, dtype=jnp.int32)
    col_ids = jnp.arange(WINDOW + block_rows, dtype=jnp.int32)
    dk_ext = jnp.zeros((WINDOW + tok_rows, head_dim), jnp.float32)
    dv_ext = jnp.zeros((WINDOW + tok_rows, head_dim), jnp.float32)
    key_pos = offset + 0 - WINDOW + col_ids
    query_pos = offset + 0 + row_ids
    gap_rows = query_pos[:, None] - key_pos[None, :]
    allowed = (gap_rows >= 0) & (gap_rows < WINDOW) & (key_pos >= 0)[None, :]
    dk_blk = jnp.zeros((WINDOW + block_rows, head_dim), jnp.float32)
    dv_blk = jnp.zeros((WINDOW + block_rows, head_dim), jnp.float32)
    dq_heads = []
    for head_index in range(local_heads):
        columns = slice(head_index * head_dim, (head_index + 1) * head_dim)
        q_blk = query[0:block_rows, columns]
        g_blk = grad_out[0:block_rows, columns]
        scores = (
            lax.dot_general(
                q_blk, keys_ext, (((1,), (1,)), ((), ())), preferred_element_type=jnp.float32
            )
            * score_scale
        )
        scores = jnp.where(allowed, scores, -jnp.inf)
        row_max = jnp.max(scores, axis=-1, keepdims=True)
        expo = jnp.exp(scores - row_max)
        probs = expo / jnp.sum(expo, axis=-1, keepdims=True)
        probs_low = probs.astype(jnp.bfloat16)
        dv_blk = dv_blk + lax.dot_general(
            probs_low, g_blk, (((0,), (0,)), ((), ())), preferred_element_type=jnp.float32
        )
        dprobs = lax.dot_general(
            g_blk, values_ext, (((1,), (1,)), ((), ())), preferred_element_type=jnp.float32
        )
        delta = jnp.sum(probs * dprobs, axis=-1, keepdims=True)
        dscores = (probs * (dprobs - delta) * score_scale).astype(jnp.bfloat16)
        dq_heads.append(
            jnp.dot(dscores, keys_ext, preferred_element_type=jnp.float32).astype(jnp.bfloat16)
        )
        dk_blk = dk_blk + lax.dot_general(
            dscores, q_blk, (((0,), (0,)), ((), ())), preferred_element_type=jnp.float32
        )
    dq_blocks = jnp.concatenate(dq_heads, axis=1)
    dk_ext = dk_ext.at[0 : WINDOW + block_rows].add(dk_blk)
    dv_ext = dv_ext.at[0 : WINDOW + block_rows].add(dv_blk)
    own_rows = return_halo(dk_ext, dv_ext, tok_rows, reach_shards)
    grad_key, grad_value = lax.psum((own_rows[0], own_rows[1]), "head")
    return (dq_blocks, grad_key, grad_value)


def solution(mesh):
    return jax.shard_map(
        on_device,
        mesh=mesh,
        in_specs=(P("seq", "head"), P("seq", None), P("seq", None), P("seq", "head")),
        out_specs=(P("seq", "head"), P("seq", None), P("seq", None)),
        check_vma=False,
    )
```

profile of v0, /device:TPU:25, one launch (start us, length us, event | category | flops | bytes accessed | tf_op | source)
XLA Modules:
  0.0 204.8 jit_solution(3855832918485448326)
XLA Ops:
  7.2 3.5 %collective-permute-start.2 = (bf16[512,256]{1,0:T(8,128)(2,1)}, bf16[512,256]{1,0:T(8,128)(2,1)S(1)}, u32[]{:S(2)}, u32[]{:S(2)}) collective-permute-start(bf16[512,256]{1,0:T(8,128)(2,1)} %param.13), channel_id=1, source_target_pairs={{0,8},{4,12},{8,16},{12,20},{16,24},{20,28},{24,32},{28,36},{32,40... | collective-permute-start | bytes 786440 | tf_op jit(solution)/shard_map/ppermute | solution.py:12
  10.8 4.5 %collective-permute-start.1 = (bf16[512,256]{1,0:T(8,128)(2,1)}, bf16[512,256]{1,0:T(8,128)(2,1)S(1)}, u32[]{:S(2)}, u32[]{:S(2)}) collective-permute-start(bf16[512,256]{1,0:T(8,128)(2,1)} %param.13), channel_id=1, source_target_pairs={{0,12},{4,16},{8,20},{12,24},{16,28},{20,32},{24,36},{28,40},{32,4... | collective-permute-start | bytes 786440 | tf_op jit(solution)/shard_map/ppermute | solution.py:12
  15.2 3.0 %collective-permute-start = (bf16[512,256]{1,0:T(8,128)(2,1)}, bf16[512,256]{1,0:T(8,128)(2,1)S(1)}, u32[]{:S(2)}, u32[]{:S(2)}) collective-permute-start(bf16[512,256]{1,0:T(8,128)(2,1)} %param.13), channel_id=1, source_target_pairs={{0,16},{4,20},{8,24},{12,28},{16,32},{20,36},{24,40},{28,44},{32,4... | collective-permute-start | bytes 786440 | tf_op jit(solution)/shard_map/ppermute | solution.py:12
  18.2 2.8 %collective-permute-start.3 = (bf16[512,256]{1,0:T(8,128)(2,1)}, bf16[512,256]{1,0:T(8,128)(2,1)S(1)}, u32[]{:S(2)}, u32[]{:S(2)}) collective-permute-start(bf16[512,256]{1,0:T(8,128)(2,1)} %param.13), channel_id=1, source_target_pairs={{0,4},{4,8},{8,12},{12,16},{16,20},{20,24},{24,28},{28,32},{32,36}... | collective-permute-start | bytes 786440 | tf_op jit(solution)/shard_map/ppermute | solution.py:12
  21.0 1.9 collective-permute-start.6
  23.0 16.2 %collective-permute-done = bf16[512,256]{1,0:T(8,128)(2,1)S(1)} collective-permute-done((bf16[512,256]{1,0:T(8,128)(2,1)}, bf16[512,256]{1,0:T(8,128)(2,1)S(1)}, u32[]{:S(2)}, u32[]{:S(2)}) %collective-permute-start) | collective-permute-done | bytes 262176 | tf_op jit(solution)/shard_map/ppermute | solution.py:12
  39.2 1.9 collective-permute-start.5
  41.1 1.9 collective-permute-start.4
  43.1 2.6 %collective-permute-start.7 = (bf16[512,256]{1,0:T(8,128)(2,1)}, bf16[512,256]{1,0:T(8,128)(2,1)S(1)}, u32[]{:S(2)}, u32[]{:S(2)}) collective-permute-start(bf16[512,256]{1,0:T(8,128)(2,1)} %param.14), channel_id=1, source_target_pairs={{0,4},{4,8},{8,12},{12,16},{16,20},{20,24},{24,28},{28,32},{32,36}... | collective-permute-start | bytes 786440 | tf_op jit(solution)/shard_map/ppermute | solution.py:12
  46.8 3.1 %fusion.64 = (f32[512]{0:T(512)S(1)}, f32[512,2560]{0,1:T(8,128)S(1)}) fusion(bf16[2560,256]{1,0:T(8,128)(2,1)S(1)} %constant_dynamic-update-slice_fusion, bf16[512,1024]{1,0:T(8,128)(2,1)} %param.12, pred[2560]{0:T(1024)(128)(4,1)S(1)} %broadcast_compare_fusion, s32[2560]{0:T(1024)S(1)} %iota_add_fusion, s32[512]{0:T(512)S(1)} %iota_add_fusion.1), kind=kOutput, calls=%fused_computation.104 | convolution fusion | flops 681573888 | bytes 6832640 | tf_op jit(solution)/shard_map/dot_general | solution.py:64
  55.6 9.7 %collective-permute-done.4 = bf16[512,256]{1,0:T(8,128)(2,1)S(1)} collective-permute-done((bf16[512,256]{1,0:T(8,128)(2,1)}, bf16[512,256]{1,0:T(8,128)(2,1)S(1)}, u32[]{:S(2)}, u32[]{:S(2)}) %collective-permute-start.4) | collective-permute-done | bytes 262176 | tf_op jit(solution)/shard_map/ppermute | solution.py:12
  67.2 3.4 %fusion.12 = (f32[512]{0:T(512)S(1)}, f32[2560,512]{1,0:T(8,128)}) fusion(f32[512]{0:T(512)S(1)} %fusion.19, f32[512,2560]{0,1:T(8,128)S(1)} %get-tuple-element.69, f32[512]{0:T(512)S(1)} %get-tuple-element.68, bf16[2560,256]{1,0:T(8,128)(2,1)S(1)} %constant_dynamic-update-slice_fusion.5, bf16[512,1024]{1,0:T(8,128)(2,1)S(1)} %copy-done.11), kind=kOutput, calls=%fused_computation.25 | convolution fusion | flops 676331008 | bytes 12064768 | tf_op jit(solution)/shard_map/dot_general | solution.py:77
  71.4 3.6 %fusion = (f32[512]{0:T(512)S(1)}, f32[2560,512]{1,0:T(8,128)}) fusion(f32[512]{0:T(512)S(1)} %fusion.25, f32[512,2560]{0,1:T(8,128)S(1)} %get-tuple-element.57, f32[512]{0:T(512)S(1)} %get-tuple-element.56, bf16[2560,256]{1,0:T(8,128)(2,1)S(1)} %constant_dynamic-update-slice_fusion.5, bf16[512,1024]{1,0:T(8,128)(2,1)S(1)} %copy-done.11), kind=kOutput, calls=%fused_computation.4 | convolution fusion | flops 676331008 | bytes 12064768 | tf_op jit(solution)/shard_map/dot_general | solution.py:77
  75.8 3.5 %fusion.4 = (f32[512]{0:T(512)S(1)}, f32[2560,512]{1,0:T(8,128)}) fusion(f32[512]{0:T(512)S(1)} %fusion.23, f32[512,2560]{0,1:T(8,128)S(1)} %get-tuple-element.61, f32[512]{0:T(512)S(1)} %get-tuple-element.60, bf16[2560,256]{1,0:T(8,128)(2,1)S(1)} %constant_dynamic-update-slice_fusion.5, bf16[512,1024]{1,0:T(8,128)(2,1)S(1)} %copy-done.11), kind=kOutput, calls=%fused_computation.11 | convolution fusion | flops 676331008 | bytes 12064768 | tf_op jit(solution)/shard_map/dot_general | solution.py:77
  80.0 3.5 %fusion.8 = (f32[512]{0:T(512)S(1)}, f32[2560,512]{1,0:T(8,128)}) fusion(f32[512]{0:T(512)S(1)} %fusion.21, f32[512,2560]{0,1:T(8,128)S(1)} %get-tuple-element.65, f32[512]{0:T(512)S(1)} %get-tuple-element.64, bf16[2560,256]{1,0:T(8,128)(2,1)S(1)} %constant_dynamic-update-slice_fusion.5, bf16[512,1024]{1,0:T(8,128)(2,1)S(1)} %copy-done.11), kind=kOutput, calls=%fused_computation.18 | convolution fusion | flops 676331008 | bytes 12064768 | tf_op jit(solution)/shard_map/dot_general | solution.py:77
  85.7 2.7 %fusion.69 = (bf16[2560,256]{1,0:T(8,128)(2,1)S(1)}, f32[2560,256]{1,0:T(8,128)}) fusion(f32[2560,256]{1,0:T(8,128)S(1)} %convolution_add_fusion.1, bf16[512,1024]{1,0:T(8,128)(2,1)S(1)} %copy-done.11, f32[512]{0:T(512)S(1)} %fusion.25, f32[512,2560]{0,1:T(8,128)S(1)} %get-tuple-element.57, f32[512]{0:T(512)S(1)} %get-tuple-element.56), kind=kOutput, calls=%fused_computation.109 | convolution fusion | flops 676331520 | bytes 12062720 | tf_op jit(solution)/shard_map/dot_general | solution.py:74
  91.2 1.9 collective-permute-start.15
  93.2 2.4 %collective-permute-start.14 = (bf16[512,256]{1,0:T(8,128)(2,1)}, bf16[512,256]{1,0:T(8,128)(2,1)}, u32[]{:S(2)}, u32[]{:S(2)}) collective-permute-start(bf16[512,256]{1,0:T(8,128)(2,1)} %get-tuple-element.50), channel_id=1, source_target_pairs={{12,0},{16,4},{20,8},{24,12},{28,16},{32,20},{36,24},{40,28},{44,3... | collective-permute-start | bytes 786440 | tf_op jit(solution)/shard_map/ppermute | solution.py:12
  95.6 2.2 %collective-permute-start.13 = (bf16[512,256]{1,0:T(8,128)(2,1)S(1)}, bf16[512,256]{1,0:T(8,128)(2,1)}, u32[]{:S(2)}, u32[]{:S(2)}) collective-permute-start(bf16[512,256]{1,0:T(8,128)(2,1)S(1)} %get-tuple-element.51), channel_id=1, source_target_pairs={{8,0},{12,4},{16,8},{20,12},{24,16},{28,20},{32,24},{36,28},{40,32... | collective-permute-start | bytes 786440 | tf_op jit(solution)/shard_map/ppermute | solution.py:12
  97.8 3.9 %fusion.15 = bf16[512,2560]{0,1:T(8,128)(2,1)S(1)} fusion(f32[2560,512]{1,0:T(8,128)} %get-tuple-element.71, f32[512]{0:T(512)S(1)} %get-tuple-element.70, f32[512]{0:T(512)S(1)} %fusion.19, f32[512,2560]{0,1:T(8,128)S(1)} %get-tuple-element.69, f32[512]{0:T(512)S(1)} %get-tuple-element.68), kind=kLoop, calls=%fused_computation.28 | loop fusion | flops 7864320 | bytes 13113344 | tf_op jit(solution)/shard_map/convert_element_type | solution.py:81
  102.6 3.9 %fusion.3 = bf16[512,2560]{0,1:T(8,128)(2,1)S(1)} fusion(f32[2560,512]{1,0:T(8,128)} %get-tuple-element.59, f32[512]{0:T(512)S(1)} %get-tuple-element.58, f32[512]{0:T(512)S(1)} %fusion.25, f32[512,2560]{0,1:T(8,128)S(1)} %get-tuple-element.57, f32[512]{0:T(512)S(1)} %get-tuple-element.56), kind=kLoop, calls=%fused_computation.7 | loop fusion | flops 7864320 | bytes 13113344 | tf_op jit(solution)/shard_map/convert_element_type | solution.py:81
  106.6 3.9 %fusion.7 = bf16[512,2560]{0,1:T(8,128)(2,1)S(1)} fusion(f32[2560,512]{1,0:T(8,128)} %get-tuple-element.63, f32[512]{0:T(512)S(1)} %get-tuple-element.62, f32[512]{0:T(512)S(1)} %fusion.23, f32[512,2560]{0,1:T(8,128)S(1)} %get-tuple-element.61, f32[512]{0:T(512)S(1)} %get-tuple-element.60), kind=kLoop, calls=%fused_computation.14 | loop fusion | flops 7864320 | bytes 13113344 | tf_op jit(solution)/shard_map/convert_element_type | solution.py:81
  110.5 4.0 %fusion.11 = bf16[512,2560]{0,1:T(8,128)(2,1)S(1)} fusion(f32[2560,512]{1,0:T(8,128)} %get-tuple-element.67, f32[512]{0:T(512)S(1)} %get-tuple-element.66, f32[512]{0:T(512)S(1)} %fusion.21, f32[512,2560]{0,1:T(8,128)S(1)} %get-tuple-element.65, f32[512]{0:T(512)S(1)} %get-tuple-element.64), kind=kLoop, calls=%fused_computation.21 | loop fusion | flops 7864320 | bytes 13113344 | tf_op jit(solution)/shard_map/convert_element_type | solution.py:81
  117.8 2.1 %collective-permute-start.8 = (bf16[512,256]{1,0:T(8,128)(2,1)S(1)}, bf16[512,256]{1,0:T(8,128)(2,1)S(1)}, u32[]{:S(2)}, u32[]{:S(2)}) collective-permute-start(bf16[512,256]{1,0:T(8,128)(2,1)S(1)} %get-tuple-element.52), channel_id=1, source_target_pairs={{4,0},{8,4},{12,8},{16,12},{20,16},{24,20},{28,24},{32,28},{36,32}... | collective-permute-start | bytes 786440 | tf_op jit(solution)/shard_map/ppermute | solution.py:12
  121.5 4.6 %collective-permute-start.11 = (bf16[512,256]{1,0:T(8,128)(2,1)S(1)}, bf16[512,256]{1,0:T(8,128)(2,1)S(1)}, u32[]{:S(2)}, u32[]{:S(2)}) collective-permute-start(bf16[512,256]{1,0:T(8,128)(2,1)S(1)} %get-tuple-element.53), channel_id=1, source_target_pairs={{16,0},{20,4},{24,8},{28,12},{32,16},{36,20},{40,24},{44,28},{48,3... | collective-permute-start | bytes 786440 | tf_op jit(solution)/shard_map/ppermute | solution.py:12
  126.1 3.1 %collective-permute-start.10 = (bf16[512,256]{1,0:T(8,128)(2,1)S(1)}, bf16[512,256]{1,0:T(8,128)(2,1)S(1)}, u32[]{:S(2)}, u32[]{:S(2)}) collective-permute-start(bf16[512,256]{1,0:T(8,128)(2,1)S(1)} %get-tuple-element.54), channel_id=1, source_target_pairs={{12,0},{16,4},{20,8},{24,12},{28,16},{32,20},{36,24},{40,28},{44,3... | collective-permute-start | bytes 786440 | tf_op jit(solution)/shard_map/ppermute | solution.py:12
  129.2 3.2 %collective-permute-start.9 = (bf16[512,256]{1,0:T(8,128)(2,1)S(1)}, bf16[512,256]{1,0:T(8,128)(2,1)S(1)}, u32[]{:S(2)}, u32[]{:S(2)}) collective-permute-start(bf16[512,256]{1,0:T(8,128)(2,1)S(1)} %get-tuple-element.55), channel_id=1, source_target_pairs={{8,0},{12,4},{16,8},{20,12},{24,16},{28,20},{32,24},{36,28},{40,32... | collective-permute-start | bytes 786440 | tf_op jit(solution)/shard_map/ppermute | solution.py:12
  132.5 2.1 %fusion.33 = f32[512,256]{1,0:T(8,128)} fusion(f32[2560,256]{1,0:T(8,128)} %get-tuple-element.75, bf16[512,256]{1,0:T(8,128)(2,1)S(1)} %collective-permute-done.15, bf16[512,256]{1,0:T(8,128)(2,1)} %collective-permute-done.14, bf16[512,256]{1,0:T(8,128)(2,1)} %collective-permute-done.13, bf16[512,256]{1,0:T(8,128)(2,1)S(1)} %collective-permute-done.12), kind=kLoop, calls=%fused_computation.63 | loop fusion | flops 1048576 | bytes 2097152 | tf_op jit(solution)/shard_map/add | solution.py:16
  134.9 8.7 %collective-permute-done.9 = bf16[512,256]{1,0:T(8,128)(2,1)S(1)} collective-permute-done((bf16[512,256]{1,0:T(8,128)(2,1)S(1)}, bf16[512,256]{1,0:T(8,128)(2,1)S(1)}, u32[]{:S(2)}, u32[]{:S(2)}) %collective-permute-start.9) | collective-permute-done | bytes 262176 | tf_op jit(solution)/shard_map/ppermute | solution.py:12
  144.6 2.4 %convolution_convert_fusion.1 = bf16[512,256]{0,1:T(8,128)(2,1)S(1)} fusion(bf16[512,2560]{0,1:T(8,128)(2,1)S(1)} %fusion.7, bf16[2560,256]{1,0:T(8,128)(2,1)} %copy-done.8), kind=kOutput, calls=%fused_computation.56 | convolution fusion | flops 671219712 | bytes 4194304 | tf_op jit(solution)/shard_map/dot_general | solution.py:83
  147.0 2.3 %convolution_convert_fusion.3 = bf16[512,256]{0,1:T(8,128)(2,1)S(1)} fusion(bf16[512,2560]{0,1:T(8,128)(2,1)S(1)} %copy-done.3, bf16[2560,256]{1,0:T(8,128)(2,1)} %copy-done.8), kind=kOutput, calls=%fused_computation.58 | convolution fusion | flops 671219712 | bytes 4194304 | tf_op jit(solution)/shard_map/dot_general | solution.py:83
  151.6 42.6 %all-reduce.3.cloned.1.call-done = (f32[512,256]{1,0:T(8,128)}, f32[512,256]{1,0:T(8,128)}) async-done(((f32[512,256]{1,0:T(8,128)}, f32[512,256]{1,0:T(8,128)}), (f32[512,256]{1,0:T(8,128)}, f32[512,256]{1,0:T(8,128)})) %all-reduce.3.cloned.1.call-update) | async-done | bytes 1048592 | tf_op jit(solution)/shard_map/psum | solution.py:92
  (76 shorter events, 28.9 us)
Async XLA Ops:
  7.2 187.0 %all-reduce.3.cloned.1.call-start = ((), (), s32[]{:S(2)}) async-start(), calls=%async_computation | async-start | bytes 2097152 | tf_op jit(solution)/shard_map/psum | solution.py:92
  7.2 35.9 %collective-permute-start.2 = (bf16[512,256]{1,0:T(8,128)(2,1)}, bf16[512,256]{1,0:T(8,128)(2,1)S(1)}, u32[]{:S(2)}, u32[]{:S(2)}) collective-permute-start(bf16[512,256]{1,0:T(8,128)(2,1)} %param.13), channel_id=1, source_target_pairs={{0,8},{4,12},{8,16},{12,20},{16,24},{20,28},{24,32},{28,36},{32,40... | collective-permute-start | bytes 786440 | tf_op jit(solution)/shard_map/ppermute | solution.py:12
  10.8 30.4 %collective-permute-start.1 = (bf16[512,256]{1,0:T(8,128)(2,1)}, bf16[512,256]{1,0:T(8,128)(2,1)S(1)}, u32[]{:S(2)}, u32[]{:S(2)}) collective-permute-start(bf16[512,256]{1,0:T(8,128)(2,1)} %param.13), channel_id=1, source_target_pairs={{0,12},{4,16},{8,20},{12,24},{16,28},{20,32},{24,36},{28,40},{32,4... | collective-permute-start | bytes 786440 | tf_op jit(solution)/shard_map/ppermute | solution.py:12
  15.2 23.9 %collective-permute-start = (bf16[512,256]{1,0:T(8,128)(2,1)}, bf16[512,256]{1,0:T(8,128)(2,1)S(1)}, u32[]{:S(2)}, u32[]{:S(2)}) collective-permute-start(bf16[512,256]{1,0:T(8,128)(2,1)} %param.13), channel_id=1, source_target_pairs={{0,16},{4,20},{8,24},{12,28},{16,32},{20,36},{24,40},{28,44},{32,4... | collective-permute-start | bytes 786440 | tf_op jit(solution)/shard_map/ppermute | solution.py:12
  18.2 27.6 %collective-permute-start.3 = (bf16[512,256]{1,0:T(8,128)(2,1)}, bf16[512,256]{1,0:T(8,128)(2,1)S(1)}, u32[]{:S(2)}, u32[]{:S(2)}) collective-permute-start(bf16[512,256]{1,0:T(8,128)(2,1)} %param.13), channel_id=1, source_target_pairs={{0,4},{4,8},{8,12},{12,16},{16,20},{20,24},{24,28},{28,32},{32,36}... | collective-permute-start | bytes 786440 | tf_op jit(solution)/shard_map/ppermute | solution.py:12
  21.0 44.3 %collective-permute-start.6 = (bf16[512,256]{1,0:T(8,128)(2,1)}, bf16[512,256]{1,0:T(8,128)(2,1)S(1)}, u32[]{:S(2)}, u32[]{:S(2)}) collective-permute-start(bf16[512,256]{1,0:T(8,128)(2,1)} %param.14), channel_id=1, source_target_pairs={{0,8},{4,12},{8,16},{12,20},{16,24},{20,28},{24,32},{28,36},{32,40... | collective-permute-start | bytes 786440 | tf_op jit(solution)/shard_map/ppermute | solution.py:12
  39.2 26.1 %collective-permute-start.5 = (bf16[512,256]{1,0:T(8,128)(2,1)}, bf16[512,256]{1,0:T(8,128)(2,1)S(1)}, u32[]{:S(2)}, u32[]{:S(2)}) collective-permute-start(bf16[512,256]{1,0:T(8,128)(2,1)} %param.14), channel_id=1, source_target_pairs={{0,12},{4,16},{8,20},{12,24},{16,28},{20,32},{24,36},{28,40},{32,4... | collective-permute-start | bytes 786440 | tf_op jit(solution)/shard_map/ppermute | solution.py:12
  41.1 24.1 %collective-permute-start.4 = (bf16[512,256]{1,0:T(8,128)(2,1)}, bf16[512,256]{1,0:T(8,128)(2,1)S(1)}, u32[]{:S(2)}, u32[]{:S(2)}) collective-permute-start(bf16[512,256]{1,0:T(8,128)(2,1)} %param.14), channel_id=1, source_target_pairs={{0,16},{4,20},{8,24},{12,28},{16,32},{20,36},{24,40},{28,44},{32,4... | collective-permute-start | bytes 786440 | tf_op jit(solution)/shard_map/ppermute | solution.py:12
  43.1 22.2 %collective-permute-start.7 = (bf16[512,256]{1,0:T(8,128)(2,1)}, bf16[512,256]{1,0:T(8,128)(2,1)S(1)}, u32[]{:S(2)}, u32[]{:S(2)}) collective-permute-start(bf16[512,256]{1,0:T(8,128)(2,1)} %param.14), channel_id=1, source_target_pairs={{0,4},{4,8},{8,12},{12,16},{16,20},{20,24},{24,28},{28,32},{32,36}... | collective-permute-start | bytes 786440 | tf_op jit(solution)/shard_map/ppermute | solution.py:12
  46.8 6.9 %copy-start.8 = (bf16[2560,256]{1,0:T(8,128)(2,1)}, bf16[2560,256]{1,0:T(8,128)(2,1)S(1)}, u32[]{:S(2)}) copy-start(bf16[2560,256]{1,0:T(8,128)(2,1)S(1)} %constant_dynamic-update-slice_fusion) | copy-start | bytes 3932164
  46.8 3.1 %copy-start.4 = (bf16[512,1024]{1,0:T(8,128)(2,1)S(1)}, bf16[512,1024]{1,0:T(8,128)(2,1)}, u32[]{:S(2)}) copy-start(bf16[512,1024]{1,0:T(8,128)(2,1)} %param.12) | copy-start | bytes 3145732
  53.7 11.7 %copy-start.6 = (bf16[512,256]{1,0:T(8,128)(2,1)S(1)}, bf16[512,256]{1,0:T(8,128)(2,1)}, u32[]{:S(2)}) copy-start(bf16[512,256]{1,0:T(8,128)(2,1)} %param.14) | copy-start | bytes 786436
  55.6 10.6 %copy-start.11 = (bf16[512,1024]{1,0:T(8,128)(2,1)S(1)}, bf16[512,1024]{1,0:T(8,128)(2,1)}, u32[]{:S(2)}) copy-start(bf16[512,1024]{1,0:T(8,128)(2,1)} %param.15) | copy-start | bytes 3145732
  89.3 32.2 %collective-permute-start.12 = (bf16[512,256]{1,0:T(8,128)(2,1)}, bf16[512,256]{1,0:T(8,128)(2,1)S(1)}, u32[]{:S(2)}, u32[]{:S(2)}) collective-permute-start(bf16[512,256]{1,0:T(8,128)(2,1)} %get-tuple-element.48), channel_id=1, source_target_pairs={{4,0},{8,4},{12,8},{16,12},{20,16},{24,20},{28,24},{32,28},{36,32}... | collective-permute-start | bytes 786440 | tf_op jit(solution)/shard_map/ppermute | solution.py:12
  91.2 34.9 %collective-permute-start.15 = (bf16[512,256]{1,0:T(8,128)(2,1)}, bf16[512,256]{1,0:T(8,128)(2,1)S(1)}, u32[]{:S(2)}, u32[]{:S(2)}) collective-permute-start(bf16[512,256]{1,0:T(8,128)(2,1)} %get-tuple-element.49), channel_id=1, source_target_pairs={{16,0},{20,4},{24,8},{28,12},{32,16},{36,20},{40,24},{44,28},{48,3... | collective-permute-start | bytes 786440 | tf_op jit(solution)/shard_map/ppermute | solution.py:12
  93.2 36.1 %collective-permute-start.14 = (bf16[512,256]{1,0:T(8,128)(2,1)}, bf16[512,256]{1,0:T(8,128)(2,1)}, u32[]{:S(2)}, u32[]{:S(2)}) collective-permute-start(bf16[512,256]{1,0:T(8,128)(2,1)} %get-tuple-element.50), channel_id=1, source_target_pairs={{12,0},{16,4},{20,8},{24,12},{28,16},{32,20},{36,24},{40,28},{44,3... | collective-permute-start | bytes 786440 | tf_op jit(solution)/shard_map/ppermute | solution.py:12
  95.6 36.9 %collective-permute-start.13 = (bf16[512,256]{1,0:T(8,128)(2,1)S(1)}, bf16[512,256]{1,0:T(8,128)(2,1)}, u32[]{:S(2)}, u32[]{:S(2)}) collective-permute-start(bf16[512,256]{1,0:T(8,128)(2,1)S(1)} %get-tuple-element.51), channel_id=1, source_target_pairs={{8,0},{12,4},{16,8},{20,12},{24,16},{28,20},{32,24},{36,28},{40,32... | collective-permute-start | bytes 786440 | tf_op jit(solution)/shard_map/ppermute | solution.py:12
  101.8 4.8 %copy-start.2 = (bf16[512,2560]{0,1:T(8,128)(2,1)}, bf16[512,2560]{0,1:T(8,128)(2,1)S(1)}, u32[]{:S(2)}) copy-start(bf16[512,2560]{0,1:T(8,128)(2,1)S(1)} %fusion.15) | copy-start | bytes 7864324
  110.5 4.0 %copy-start.5 = (bf16[512,1024]{1,0:T(8,128)(2,1)S(1)}, bf16[512,1024]{1,0:T(8,128)(2,1)}, u32[]{:S(2)}) copy-start(bf16[512,1024]{1,0:T(8,128)(2,1)} %param.12) | copy-start | bytes 3145732
  114.5 1.5 copy-start
  116.9 3.1 %copy-start.9 = (bf16[2560,256]{1,0:T(8,128)(2,1)S(1)}, bf16[2560,256]{1,0:T(8,128)(2,1)}, u32[]{:S(2)}) copy-start(bf16[2560,256]{1,0:T(8,128)(2,1)} %copy-done.8) | copy-start | bytes 3932164
  117.8 16.8 %collective-permute-start.8 = (bf16[512,256]{1,0:T(8,128)(2,1)S(1)}, bf16[512,256]{1,0:T(8,128)(2,1)S(1)}, u32[]{:S(2)}, u32[]{:S(2)}) collective-permute-start(bf16[512,256]{1,0:T(8,128)(2,1)S(1)} %get-tuple-element.52), channel_id=1, source_target_pairs={{4,0},{8,4},{12,8},{16,12},{20,16},{24,20},{28,24},{32,28},{36,32}... | collective-permute-start | bytes 786440 | tf_op jit(solution)/shard_map/ppermute | solution.py:12
  121.5 13.1 %collective-permute-start.11 = (bf16[512,256]{1,0:T(8,128)(2,1)S(1)}, bf16[512,256]{1,0:T(8,128)(2,1)S(1)}, u32[]{:S(2)}, u32[]{:S(2)}) collective-permute-start(bf16[512,256]{1,0:T(8,128)(2,1)S(1)} %get-tuple-element.53), channel_id=1, source_target_pairs={{16,0},{20,4},{24,8},{28,12},{32,16},{36,20},{40,24},{44,28},{48,3... | collective-permute-start | bytes 786440 | tf_op jit(solution)/shard_map/ppermute | solution.py:12
  126.1 8.8 %collective-permute-start.10 = (bf16[512,256]{1,0:T(8,128)(2,1)S(1)}, bf16[512,256]{1,0:T(8,128)(2,1)S(1)}, u32[]{:S(2)}, u32[]{:S(2)}) collective-permute-start(bf16[512,256]{1,0:T(8,128)(2,1)S(1)} %get-tuple-element.54), channel_id=1, source_target_pairs={{12,0},{16,4},{20,8},{24,12},{28,16},{32,20},{36,24},{40,28},{44,3... | collective-permute-start | bytes 786440 | tf_op jit(solution)/shard_map/ppermute | solution.py:12
  129.2 14.4 %collective-permute-start.9 = (bf16[512,256]{1,0:T(8,128)(2,1)S(1)}, bf16[512,256]{1,0:T(8,128)(2,1)S(1)}, u32[]{:S(2)}, u32[]{:S(2)}) collective-permute-start(bf16[512,256]{1,0:T(8,128)(2,1)S(1)} %get-tuple-element.55), channel_id=1, source_target_pairs={{8,0},{12,4},{16,8},{20,12},{24,16},{28,20},{32,24},{36,28},{40,32... | collective-permute-start | bytes 786440 | tf_op jit(solution)/shard_map/ppermute | solution.py:12
  144.6 2.4 %copy-start.3 = (bf16[512,2560]{0,1:T(8,128)(2,1)S(1)}, bf16[512,2560]{0,1:T(8,128)(2,1)}, u32[]{:S(2)}) copy-start(bf16[512,2560]{0,1:T(8,128)(2,1)} %copy-done.2) | copy-start | bytes 7864324
  144.6 4.7 %copy-start.1 = (bf16[512,2560]{0,1:T(8,128)(2,1)S(1)}, bf16[512,2560]{0,1:T(8,128)(2,1)}, u32[]{:S(2)}) copy-start(bf16[512,2560]{0,1:T(8,128)(2,1)} %copy-done) | copy-start | bytes 7864324
  144.6 4.7 %copy-start.10 = (bf16[2560,256]{1,0:T(8,128)(2,1)S(1)}, bf16[2560,256]{1,0:T(8,128)(2,1)}, u32[]{:S(2)}) copy-start(bf16[2560,256]{1,0:T(8,128)(2,1)} %copy-done.8) | copy-start | bytes 3932164
  147.0 3.2 %copy-start.7 = (bf16[512,256]{0,1:T(8,128)(2,1)S(1)}, bf16[512,256]{0,1:T(8,128)(2,1)}, u32[]{:S(2)}) copy-start(bf16[512,256]{0,1:T(8,128)(2,1)} %convolution_convert_fusion) | copy-start | bytes 786436
Sparse Core Ops, SparseCore 0:
  144.7 49.3 all-reduce.2
where the time goes:
time: 207 us; the launch traced here: 205 us
  waiting for transfers between devices  77.5 us (37%)
  starting transfers between devices  43.7 us (21%)
  matrix products  39.1 us (19%)
  other arithmetic  22.1 us (11%)
  between operations  14.6 us (7%)
  local copies, waits for them, and re-layouts  7.82 us (4%)
    ppermute x16, starting transfers between devices, passed_along(): return lax.ppermute(block, axis, route)  43.6 us
    psum x1, waiting for transfers between devices, on_device(): grad_key, grad_value = lax.psum((own_rows[0], own_rows[1]), 'head')  42.6 us
    ppermute x16, waiting for transfers between devices, passed_along(): return lax.ppermute(block, axis, route)  34.9 us
    convert_element_type x4, other arithmetic, on_device(): dscores = (probs * (dprobs - delta) * score_scale).astype(jnp.bfloat16)  15.8 us
    dot_general x4, matrix products, on_device(): lax.dot_general(g_blk, values_ext, (((1,), (1,)), ((), ())), preferred_el...  14 us
    dot_general x4, matrix products, on_device(): lax.dot_general(q_blk, keys_ext, (((1,), (1,)), ((), ())), preferred_elem...  8.71 us
    dot_general x4, matrix products, on_device(): jnp.dot(dscores, keys_ext, preferred_element_type=jnp.float32)  7.09 us
    dot_general x4, matrix products, on_device(): lax.dot_general(probs_low, g_blk, (((0,), (0,)), ((), ())), preferred_ele...  5.96 us
  transfers between devices with their start and end apart: 17, of which 5 were waited for; matrix products, arithmetic and copies ran while one was open for 19% of the time, Pallas kernels for 0%

commit v1 on v0

v1 whole, which is shorter than its diff:
```python
import jax
import jax.numpy as jnp
from jax import lax
from jax.experimental import pallas as pl
from jax.experimental.pallas import tpu as pltpu
from jax.sharding import PartitionSpec as P

F32 = jnp.float32
BF16 = jnp.bfloat16
MESH = pl.DeviceIdType.MESH
REACH = 4
LOG2E = 1.4426950408889634
NEG = -1e30
NT = (((1,), (1,)), ((), ()))
NN = (((1,), (0,)), ((), ()))
TN = (((0,), (0,)), ((), ()))


def kernel(
    q_hbm, g_hbm, k_hbm, v_hbm,
    dq_out, fin_out,
    q_ref, g_ref, kv, e_ref, dp_ref, md, m_run, l_run, dl_run, ds_low, dq_acc,
    acc, pair_send, pair_recv, half_keep, half_send, half_recv,
    quart_send, quart_recv, own_quart, fin,
    load_sem, send_sem, net_sem, mate_sem, pair_sem, half_sem, quart_sem, fin_sem,
):
    tok, dh = kv.shape[2], kv.shape[3]
    heads = e_ref.shape[1]
    hb = tok // 2
    scale = dh ** (-0.5)
    to_log2 = scale * LOG2E
    n_seq = lax.axis_size("seq")
    s, hd = lax.axis_index("seq"), lax.axis_index("head")
    xl, xh, c = lax.rem(s, 2), lax.div(hd, 2), lax.rem(hd, 2)
    opp = s + 1 - 2 * xl
    mate = (s, hd + 1 - 2 * c)
    across = (s, lax.rem(hd + 2, 4))

    def half(index):
        return pl.ds(pl.multiple_of(index * hb, hb), hb)

    loads = [
        pltpu.make_async_copy(src, dst, load_sem.at[i])
        for i, (src, dst) in enumerate(
            ((k_hbm, kv.at[0, 0]), (v_hbm, kv.at[0, 1]), (q_hbm, q_ref), (g_hbm, g_ref))
        )
    ]
    for load in loads:
        load.start()
    barrier = pltpu.get_barrier_semaphore()

    def greet(device):
        pl.semaphore_signal(barrier, inc=1, device_id=device, device_id_type=MESH)

    for head in (hd, across[1]):
        greet((opp, head))
    greet(mate)
    greet(across)
    for d in range(1, REACH + 1):
        @pl.when(s + d < n_seq)
        def _(d=d):
            greet((s + d, hd))

        @pl.when(s >= d)
        def _(d=d):
            greet((s - d, hd))
    ahead = jnp.minimum(n_seq - 1 - s, REACH)
    behind = jnp.minimum(s, REACH)
    pl.semaphore_wait(barrier, 4 + ahead + behind)
    for load in loads:
        load.wait()

    pending = []

    def send(cond, src, dst, recv_sem, device):
        copy = pltpu.make_async_remote_copy(
            src_ref=src, dst_ref=dst, send_sem=send_sem.at[len(pending)], recv_sem=recv_sem,
            device_id=device, device_id_type=MESH,
        )
        pending.append((cond, copy))

        @pl.when(cond)
        def _():
            copy.start()

    def arrived(buf, sem):
        pltpu.make_async_remote_copy(
            src_ref=buf, dst_ref=buf, send_sem=send_sem.at[0], recv_sem=sem,
            device_id=mate, device_id_type=MESH,
        ).wait_recv()

    def when_arrived(cond, buf, sem):
        @pl.when(cond)
        def _():
            arrived(buf, sem)

    def kv_half(d, array, index):
        return kv.at[d, array, half(index), :]

    def over_x(cond, src_slot, dst_slot):
        for x_hi in range(2):
            send(
                cond, kv_half(src_slot, c, xh), kv_half(dst_slot, c, xh), net_sem.at[dst_slot, xh],
                (opp, 2 * x_hi + c),
            )

    def to_mate(cond, d, index):
        send(cond, kv_half(d, c, index), kv_half(d, c, index), mate_sem.at[d, index], mate)

    order = (xh, 1 - xh)
    for index in order:
        send(s + 2 < n_seq, kv_half(0, c, index), kv_half(2, c, index), net_sem.at[2, index], (s + 2, hd))
        if index is order[0]:
            over_x(xl == 0, 0, 1)

    def relay_two(j):
        index = order[j]
        when_arrived(s >= 2, kv_half(2, c, index), net_sem.at[2, index])
        send(
            (s >= 2) & (s + 2 < n_seq), kv_half(2, c, index), kv_half(4, c, index), net_sem.at[4, index],
            (s + 2, hd),
        )
        if j == 0:
            over_x(s >= 2, 2, 3 - 2 * xl)
        to_mate(s >= 2, 2, index)

    def relay_four(j):
        index = order[j]
        when_arrived(s >= 4, kv_half(4, c, index), net_sem.at[4, index])
        if j == 0:
            over_x((s >= 4) & (xl == 1), 4, 3)
        to_mate(s >= 4, 4, index)

    def relay_odd(cond, d):
        for index in range(2):
            when_arrived(cond, kv_half(d, c, index), net_sem.at[d, index])
            to_mate(cond, d, index)

    def mate_ready(d):
        for index in range(2):
            arrived(kv_half(d, 1 - c, index), mate_sem.at[d, index])

    def key_range(d, qc):
        if d == 0:
            return 0, hb * (qc + 1)
        if d == REACH:
            return hb * qc, tok
        return 0, tok

    def query_range(d, kc):
        if d == 0:
            return hb * kc, tok
        if d == REACH:
            return 0, hb * (kc + 1)
        return 0, tok

    def scores_of(d):
        def body(h, carry):
            cols = pl.ds(pl.multiple_of(h * dh, dh), dh)
            for qc in range(2):
                k0, k1 = key_range(d if isinstance(d, int) else 1, qc)
                qs = slice(qc * hb, (qc + 1) * hb)
                logits = to_log2 * lax.dot_general(
                    kv[d, 0, k0:k1, :], q_ref[qs, cols], NT, preferred_element_type=F32
                )
                dprobs = lax.dot_general(
                    kv[d, 1, k0:k1, :], g_ref[qs, cols], NT, preferred_element_type=F32
                )
                first = isinstance(d, int) and d == 0
                if isinstance(d, int):
                    row = lax.broadcasted_iota(jnp.int32, logits.shape, 0) + k0
                    col = lax.broadcasted_iota(jnp.int32, logits.shape, 1) + qc * hb
                    logits = jnp.where((row <= col) if d == 0 else (row > col), logits, NEG)
                top = jnp.max(logits, axis=0, keepdims=True)
                if not first:
                    before = m_run[h, :, qs]
                    top = jnp.maximum(before, top)
                expo = jnp.exp2(logits - top)
                total = jnp.sum(expo, axis=0, keepdims=True)
                dots = jnp.sum(expo * dprobs, axis=0, keepdims=True)
                e_ref[d, h, k0:k1, qs] = expo
                dp_ref[d, h, k0:k1, qs] = dprobs
                md[d, h, :, qs] = top
                if not first:
                    fade = jnp.exp2(before - top)
                    total += l_run[h, :, qs] * fade
                    dots += dl_run[h, :, qs] * fade
                m_run[h, :, qs] = top
                l_run[h, :, qs] = total
                dl_run[h, :, qs] = dots
            return carry

        lax.fori_loop(0, heads, body, 0)

    scores_of(0)
    dq_acc[...] = jnp.zeros_like(dq_acc)
    relay_two(0)
    relay_odd(xl == 1, 1)

    @pl.when(xl == 1)
    def _():
        mate_ready(1)
        scores_of(s * 0 + 1)

    relay_two(1)
    odd_second = 1 + 2 * xl
    relay_odd(s >= odd_second, odd_second)

    @pl.when(s >= 2)
    def _():
        mate_ready(2)
        scores_of(s * 0 + 2)

    relay_four(0)

    @pl.when(s >= odd_second)
    def _():
        mate_ready(odd_second)
        scores_of(odd_second)

    relay_four(1)

    @pl.when(s >= 4)
    def _():
        mate_ready(4)
        scores_of(4)

    relay_odd((xl == 0) & (s >= 4), 3)

    @pl.when((xl == 0) & (s >= 4))
    def _():
        mate_ready(3)
        scores_of(s * 0 + 3)

    inverse = 1.0 / l_run[...]
    dl_run[...] = dl_run[...] * inverse
    l_run[...] = inverse

    def grads_of(d, into):
        static = isinstance(d, int)
        acc[into] = jnp.zeros_like(acc[into])

        def body(h, carry):
            cols = pl.ds(pl.multiple_of(h * dh, dh), dh)
            weight = jnp.exp2(md[d, h] - m_run[h]) * l_run[h]
            delta = dl_run[h]
            for kc in range(2):
                q0, q1 = query_range(d if static else 1, kc)
                ks, qs = slice(kc * hb, (kc + 1) * hb), slice(q0, q1)
                probs = e_ref[d, h, ks, qs] * weight[:, q0:q1]
                dscores = probs * (dp_ref[d, h, ks, qs] - delta[:, q0:q1])
                probs_low, dscores_low = probs.astype(BF16), dscores.astype(BF16)
                ds_low[ks, qs] = dscores_low
                acc[into, 1, ks, :] += lax.dot_general(
                    probs_low, g_ref[qs, cols], NN, preferred_element_type=F32
                )
                acc[into, 0, ks, :] += lax.dot_general(
                    dscores_low, q_ref[qs, cols], NN, preferred_element_type=F32
                )
            for qc in range(2):
                k0, k1 = key_range(d if static else 1, qc)
                qs = slice(qc * hb, (qc + 1) * hb)
                dq_acc[h, qs, :] += lax.dot_general(
                    ds_low[k0:k1, qs], kv[d, 0, k0:k1, :], TN, preferred_element_type=F32
                )
            return carry

        lax.fori_loop(0, heads, body, 0)
        acc[into, 0] = acc[into, 0] * scale

    def pair_out(d):
        @pl.when(s >= d)
        def _():
            pair_send[d] = acc[d % 2, 1 - c].astype(BF16)

        send(s >= d, pair_send.at[d], pair_recv.at[d], pair_sem.at[d], mate)

    def half_out(d):
        @pl.when(s >= d)
        def _():
            arrived(pair_recv.at[d], pair_sem.at[d])
            there, here = half(1 - xh), half(xh)
            half_send[d] = (acc[d % 2, c, there, :] + pair_recv[d, there, :].astype(F32)).astype(BF16)
            half_keep[d] = acc[d % 2, c, here, :] + pair_recv[d, here, :].astype(F32)

        send(s >= d, half_send.at[d], half_recv.at[d], half_sem.at[d], across)

    def quarter_out(d):
        @pl.when(s >= d)
        def _():
            arrived(half_recv.at[d], half_sem.at[d])
            mine = half_keep[d] + half_recv[d].astype(F32)
            if d:
                quart_send[d - 1] = mine.astype(BF16)
            else:
                own_quart[...] = mine

        if d:
            send(s >= d, quart_send.at[d - 1], quart_recv.at[d - 1], quart_sem.at[d - 1], (s - d, hd))

    for d in range(REACH, -1, -1):
        @pl.when(s >= d)
        def _(d=d):
            grads_of(d if d in (0, REACH) else s * 0 + d, d % 2)

        pair_out(d)
        if d + 1 <= REACH:
            half_out(d + 1)
        if d + 2 <= REACH:
            quarter_out(d + 2)
    for h in range(heads):
        dq_out[:, h * dh : (h + 1) * dh] = (dq_acc[h] * scale).astype(BF16)
    half_out(0)
    quarter_out(1)
    quarter_out(0)
    for d in range(REACH, 0, -1):
        @pl.when(s + d < n_seq)
        def _(d=d):
            arrived(quart_recv.at[d - 1], quart_sem.at[d - 1])
            own_quart[...] += quart_recv[d - 1].astype(F32)

    def fin_half(array, index):
        return fin.at[array, half(index), :]

    fin[c, half(xh), :] = own_quart[...].astype(BF16)
    always = s >= 0
    send(always, fin_half(c, xh), fin_half(c, xh), fin_sem.at[0], across)
    send(always, fin_half(c, xh), fin_half(c, xh), fin_sem.at[1], mate)
    arrived(fin_half(c, 1 - xh), fin_sem.at[0])
    send(always, fin_half(c, 1 - xh), fin_half(c, 1 - xh), fin_sem.at[2], mate)
    arrived(fin_half(1 - c, xh), fin_sem.at[1])
    arrived(fin_half(1 - c, 1 - xh), fin_sem.at[2])
    fin_out[...] = fin[...]
    for cond, copy in pending:
        @pl.when(cond)
        def _(copy=copy):
            copy.wait_send()


def on_device(query, key_rows, value_rows, grad_out):
    tok, dh = key_rows.shape
    heads = query.shape[1] // dh
    blocks = REACH + 1
    vmem = pltpu.VMEM
    dma = pltpu.SemaphoreType.DMA
    grad_query, fin = pl.pallas_call(
        kernel,
        out_shape=(
            jax.ShapeDtypeStruct(query.shape, BF16),
            jax.ShapeDtypeStruct((2, tok, dh), BF16),
        ),
        in_specs=[pl.BlockSpec(memory_space=pl.ANY)] * 4,
        out_specs=(pl.BlockSpec(memory_space=vmem),) * 2,
        scratch_shapes=[
            vmem((tok, heads * dh), BF16),
            vmem((tok, heads * dh), BF16),
            vmem((blocks, 2, tok, dh), BF16),
            vmem((blocks, heads, tok, tok), F32),
            vmem((blocks, heads, tok, tok), F32),
            vmem((blocks, heads, 1, tok), F32),
            vmem((heads, 1, tok), F32),
            vmem((heads, 1, tok), F32),
            vmem((heads, 1, tok), F32),
            vmem((tok, tok), BF16),
            vmem((heads, tok, dh), F32),
            vmem((2, 2, tok, dh), F32),
            vmem((blocks, tok, dh), BF16),
            vmem((blocks, tok, dh), BF16),
            vmem((blocks, tok // 2, dh), F32),
            vmem((blocks, tok // 2, dh), BF16),
            vmem((blocks, tok // 2, dh), BF16),
            vmem((REACH, tok // 2, dh), BF16),
            vmem((REACH, tok // 2, dh), BF16),
            vmem((tok // 2, dh), F32),
            vmem((2, tok, dh), BF16),
            dma((4,)),
            dma((64,)),
            dma((blocks, 2)),
            dma((blocks, 2)),
            dma((blocks,)),
            dma((blocks,)),
            dma((REACH,)),
            dma((3,)),
        ],
        compiler_params=pltpu.CompilerParams(
            collective_id=0, has_side_effects=True, vmem_limit_bytes=67043328
        ),
    )(query, grad_out, key_rows, value_rows)
    return grad_query, fin[0].astype(F32), fin[1].astype(F32)


def solution(mesh):
    return jax.shard_map(
        on_device,
        mesh=mesh,
        in_specs=(P("seq", "head"), P("seq", None), P("seq", None), P("seq", "head")),
        out_specs=(P("seq", "head"), P("seq", None), P("seq", None)),
        check_vma=False,
    )
```

time: 207 us -> 71.4 us (0.34)
  the two profiles are of different devices: /device:TPU:25 before, /device:TPU:31 now
where the time goes in v1:
time: 71.4 us; the launch traced here: 71.3 us
  Pallas kernels  67.5 us (95%)
  other arithmetic  2.16 us (3%)
  local copies, waits for them, and re-layouts  0.97 us (1%)
    pallas_call x1, Pallas kernels, on_device(): pl.pallas_call(kernel, out_shape=(jax.ShapeDtypeStruct(query.shape, BF16)...  67.5 us
    convert_element_type x1, other arithmetic, on_device(): return (grad_query, fin[0].astype(F32), fin[1].astype(F32))  2.16 us

profile of v1, /device:TPU:31, one launch (start us, length us, event | category | flops | bytes accessed | tf_op | source)
XLA Modules:
  0.0 71.3 jit_solution(9298443701037508707)
XLA Ops:
  0.6 67.5 %shard_map.67 = (bf16[512,1024]{1,0:T(8,128)(2,1)}, bf16[2,512,256]{2,1,0:T(8,128)(2,1)}) custom-call(bf16[512,1024]{1,0:T(8,128)(2,1)} %q_hbm.1, bf16[512,1024]{1,0:T(8,128)(2,1)} %g_hbm.1, bf16[512,256]{1,0:T(8,128)(2,1)} %k_hbm.1, bf16[512,256]{1,0:T(8,128)(2,1)} %v_hbm.1), custom_call_target="tpu_custom_call" | custom-call | tf_op jit(solution)/shard_map/pallas_call | solution.py:346
  68.1 0.0 copy-start
  68.1 2.2 %bitcast_convert_fusion = (f32[512,256]{1,0:T(8,128)}, f32[512,256]{1,0:T(8,128)}) fusion(bf16[2,512,256]{2,1,0:T(8,128)(2,1)} %get-tuple-element.6), kind=kLoop, calls=%fused_computation | loop fusion | flops 262144 | bytes 1572864 | tf_op jit(solution)/shard_map/convert_element_type | solution.py:389
  70.3 0.0 copy-done
  70.3 1.0 %copy.8 = bf16[512,1024]{1,0:T(8,128)(2,1)} copy(bf16[512,1024]{1,0:T(8,128)(2,1)S(1)} %copy-done) | data formatting | bytes 2097152
Async XLA Ops:
  68.1 2.2 %copy-start = (bf16[512,1024]{1,0:T(8,128)(2,1)S(1)}, bf16[512,1024]{1,0:T(8,128)(2,1)}, u32[]{:S(2)}) copy-start(bf16[512,1024]{1,0:T(8,128)(2,1)} %get-tuple-element.12) | copy-start | bytes 3145732

commit v2 on v1

--- a/solution.py
+++ b/solution.py
@@ -19,14 +19,15 @@
 def kernel(
     q_hbm, g_hbm, k_hbm, v_hbm,
     dq_out, fin_out,
-    q_ref, g_ref, kv, e_ref, dp_ref, md, m_run, l_run, dl_run, ds_low, dq_acc,
+    q_ref, g_ref, kv, e_ref, ds_ref, md, m_run, l_run, dl_run, dq_ref,
     acc, pair_send, pair_recv, half_keep, half_send, half_recv,
     quart_send, quart_recv, own_quart, fin,
     load_sem, send_sem, net_sem, mate_sem, pair_sem, half_sem, quart_sem, fin_sem,
 ):
-    tok, dh = kv.shape[2], kv.shape[3]
+    tok, dh = e_ref.shape[2], kv.shape[2]
     heads = e_ref.shape[1]
     hb = tok // 2
+    blocks = REACH + 1
     scale = dh ** (-0.5)
     to_log2 = scale * LOG2E
     n_seq = lax.axis_size("seq")
@@ -42,7 +43,7 @@
     loads = [
         pltpu.make_async_copy(src, dst, load_sem.at[i])
         for i, (src, dst) in enumerate(
-            ((k_hbm, kv.at[0, 0]), (v_hbm, kv.at[0, 1]), (q_hbm, q_ref), (g_hbm, g_ref))
+            ((k_hbm, kv.at[0, :tok]), (v_hbm, kv.at[1, :tok]), (q_hbm, q_ref), (g_hbm, g_ref))
         )
     ]
     for load in loads:
@@ -73,15 +74,25 @@
     pending = []
 
     def send(cond, src, dst, recv_sem, device):
-        copy = pltpu.make_async_remote_copy(
-            src_ref=src, dst_ref=dst, send_sem=send_sem.at[len(pending)], recv_sem=recv_sem,
-            device_id=device, device_id_type=MESH,
-        )
-        pending.append((cond, copy))
-
-        @pl.when(cond)
+        sem = send_sem.at[len(pending)]
+        pending.append((cond, src.shape[0]))
+
+        @pl.when(cond())
         def _():
-            copy.start()
+            pltpu.make_async_remote_copy(
+                src_ref=src, dst_ref=dst, send_sem=sem, recv_sem=recv_sem,
+                device_id=device, device_id_type=MESH,
+            ).start()
+
+    def wait_sent():
+        for i, (cond, size) in enumerate(pending):
+            @pl.when(cond())
+            def _(i=i, size=size):
+                buf = pair_send.at[0, :size]
+                pltpu.make_async_remote_copy(
+                    src_ref=buf, dst_ref=buf, send_sem=send_sem.at[i], recv_sem=fin_sem.at[0],
+                    device_id=mate, device_id_type=MESH,
+                ).wait_send()
 
     def arrived(buf, sem):
         pltpu.make_async_remote_copy(
@@ -90,12 +101,12 @@
         ).wait_recv()
 
     def when_arrived(cond, buf, sem):
-        @pl.when(cond)
+        @pl.when(cond())
         def _():
             arrived(buf, sem)
 
     def kv_half(d, array, index):
-        return kv.at[d, array, half(index), :]
+        return kv.at[array, pl.ds(pl.multiple_of(d * tok + index * hb, hb), hb), :]
 
     def over_x(cond, src_slot, dst_slot):
         for x_hi in range(2):
@@ -109,27 +120,30 @@
 
     order = (xh, 1 - xh)
     for index in order:
-        send(s + 2 < n_seq, kv_half(0, c, index), kv_half(2, c, index), net_sem.at[2, index], (s + 2, hd))
+        send(lambda: s + 2 < n_seq, kv_half(0, c, index), kv_half(2, c, index), net_sem.at[2, index], (s + 2, hd))
         if index is order[0]:
-            over_x(xl == 0, 0, 1)
-
-    def relay_two(j):
+            over_x(lambda: xl == 0, 0, 1)
+
+    def relay_two(j, parity=None):
+        def here():
+            return (s >= 2) if parity is None else (s >= 2) & (xl == parity)
+
         index = order[j]
-        when_arrived(s >= 2, kv_half(2, c, index), net_sem.at[2, index])
+        when_arrived(here, kv_half(2, c, index), net_sem.at[2, index])
         send(
-            (s >= 2) & (s + 2 < n_seq), kv_half(2, c, index), kv_half(4, c, index), net_sem.at[4, index],
-            (s + 2, hd),
+            lambda: here() & (s + 2 < n_seq), kv_half(2, c, index), kv_half(4, c, index),
+            net_sem.at[4, index], (s + 2, hd),
         )
         if j == 0:
-            over_x(s >= 2, 2, 3 - 2 * xl)
-        to_mate(s >= 2, 2, index)
+            over_x(here, 2, 3 - 2 * xl)
+        to_mate(here, 2, index)
 
     def relay_four(j):
         index = order[j]
-        when_arrived(s >= 4, kv_half(4, c, index), net_sem.at[4, index])
+        when_arrived(lambda: s >= 4, kv_half(4, c, index), net_sem.at[4, index])
         if j == 0:
-            over_x((s >= 4) & (xl == 1), 4, 3)
-        to_mate(s >= 4, 4, index)
+            over_x(lambda: (s >= 4) & (xl == 1), 4, 3)
+        to_mate(lambda: s >= 4, 4, index)
 
     def relay_odd(cond, d):
         for index in range(2):
@@ -154,34 +168,45 @@
             return 0, hb * (kc + 1)
         return 0, tok
 
-    def scores_of(d):
+    def rows_of(d, k0, k1):
+        return pl.ds(pl.multiple_of(d * tok + k0, hb), k1 - k0)
+
+    def run_hooks(h, hooks):
+        for at, steps in hooks.items():
+            @pl.when(h == at)
+            def _(steps=steps):
+                for step in steps:
+                    step()
+
+    def scores_of(d, kind, hooks):
         def body(h, carry):
+            run_hooks(h, hooks)
             cols = pl.ds(pl.multiple_of(h * dh, dh), dh)
             for qc in range(2):
-                k0, k1 = key_range(d if isinstance(d, int) else 1, qc)
+                k0, k1 = key_range(kind, qc)
+                rows = rows_of(d, k0, k1)
                 qs = slice(qc * hb, (qc + 1) * hb)
                 logits = to_log2 * lax.dot_general(
-                    kv[d, 0, k0:k1, :], q_ref[qs, cols], NT, preferred_element_type=F32
+                    kv[0, rows, :], q_ref[qs, cols], NT, preferred_element_type=F32
                 )
                 dprobs = lax.dot_general(
-                    kv[d, 1, k0:k1, :], g_ref[qs, cols], NT, preferred_element_type=F32
+                    kv[1, rows, :], g_ref[qs, cols], NT, preferred_element_type=F32
                 )
-                first = isinstance(d, int) and d == 0
-                if isinstance(d, int):
+                if kind in (0, REACH):
                     row = lax.broadcasted_iota(jnp.int32, logits.shape, 0) + k0
                     col = lax.broadcasted_iota(jnp.int32, logits.shape, 1) + qc * hb
-                    logits = jnp.where((row <= col) if d == 0 else (row > col), logits, NEG)
+                    logits = jnp.where((row <= col) if kind == 0 else (row > col), logits, NEG)
                 top = jnp.max(logits, axis=0, keepdims=True)
-                if not first:
+                if kind:
                     before = m_run[h, :, qs]
                     top = jnp.maximum(before, top)
                 expo = jnp.exp2(logits - top)
                 total = jnp.sum(expo, axis=0, keepdims=True)
                 dots = jnp.sum(expo * dprobs, axis=0, keepdims=True)
                 e_ref[d, h, k0:k1, qs] = expo
-                dp_ref[d, h, k0:k1, qs] = dprobs
+                ds_ref[h, rows, qs] = dprobs
                 md[d, h, :, qs] = top
-                if not first:
+                if kind:
                     fade = jnp.exp2(before - top)
                     total += l_run[h, :, qs] * fade
                     dots += dl_run[h, :, qs] * fade
@@ -192,88 +217,102 @@
 
         lax.fori_loop(0, heads, body, 0)
 
-    scores_of(0)
-    dq_acc[...] = jnp.zeros_like(dq_acc)
+    scores_of(0, 0, {})
+    for d in range(1, REACH + 1):
+        @pl.when(s < d)
+        def _(d=d):
+            kv[0, d * tok : (d + 1) * tok, :] = jnp.zeros((tok, dh), BF16)
+            for h in range(heads):
+                ds_ref[h, d * tok : (d + 1) * tok, :] = jnp.zeros((tok, tok), F32)
+
     relay_two(0)
-    relay_odd(xl == 1, 1)
+    relay_odd(lambda: xl == 1, 1)
+    odd_second = 1 + 2 * xl
+    late = (xl == 0) & (s >= 4)
 
     @pl.when(xl == 1)
     def _():
         mate_ready(1)
-        scores_of(s * 0 + 1)
-
-    relay_two(1)
-    odd_second = 1 + 2 * xl
-    relay_odd(s >= odd_second, odd_second)
+        scores_of(1, 1, {2: [lambda: relay_two(1, 1)]})
+
+    relay_two(1, 0)
 
     @pl.when(s >= 2)
     def _():
         mate_ready(2)
-        scores_of(s * 0 + 2)
-
-    relay_four(0)
+        scores_of(2, 2, {1: [lambda: relay_odd(lambda: s >= odd_second, odd_second)], 3: [lambda: relay_four(0)]})
 
     @pl.when(s >= odd_second)
     def _():
         mate_ready(odd_second)
-        scores_of(odd_second)
-
-    relay_four(1)
+        scores_of(odd_second, 1, {3: [lambda: relay_four(1)]})
 
     @pl.when(s >= 4)
     def _():
         mate_ready(4)
-        scores_of(4)
-
-    relay_odd((xl == 0) & (s >= 4), 3)
-
-    @pl.when((xl == 0) & (s >= 4))
+        scores_of(4, 4, {2: [lambda: relay_odd(lambda: (xl == 0) & (s >= 4), 3)]})
+
+    @pl.when(late)
     def _():
         mate_ready(3)
-        scores_of(s * 0 + 3)
+        scores_of(3, 3, {})
 
     inverse = 1.0 / l_run[...]
     dl_run[...] = dl_run[...] * inverse
     l_run[...] = inverse
 
-    def grads_of(d, into):
-        static = isinstance(d, int)
+    def grads_of(d, hooks):
+        into = d % 2
         acc[into] = jnp.zeros_like(acc[into])
 
         def body(h, carry):
+            run_hooks(h, hooks)
             cols = pl.ds(pl.multiple_of(h * dh, dh), dh)
             weight = jnp.exp2(md[d, h] - m_run[h]) * l_run[h]
             delta = dl_run[h]
             for kc in range(2):
-                q0, q1 = query_range(d if static else 1, kc)
+                q0, q1 = query_range(d, kc)
                 ks, qs = slice(kc * hb, (kc + 1) * hb), slice(q0, q1)
+                rows = slice(d * tok + kc * hb, d * tok + (kc + 1) * hb)
                 probs = e_ref[d, h, ks, qs] * weight[:, q0:q1]
-                dscores = probs * (dp_ref[d, h, ks, qs] - delta[:, q0:q1])
+                dscores = probs * (ds_ref[h, rows, qs] - delta[:, q0:q1])
                 probs_low, dscores_low = probs.astype(BF16), dscores.astype(BF16)
-                ds_low[ks, qs] = dscores_low
+                ds_ref[h, rows, qs] = dscores
                 acc[into, 1, ks, :] += lax.dot_general(
                     probs_low, g_ref[qs, cols], NN, preferred_element_type=F32
                 )
                 acc[into, 0, ks, :] += lax.dot_general(
                     dscores_low, q_ref[qs, cols], NN, preferred_element_type=F32
                 )
-            for qc in range(2):
-                k0, k1 = key_range(d if static else 1, qc)
-                qs = slice(qc * hb, (qc + 1) * hb)
-                dq_acc[h, qs, :] += lax.dot_general(
-                    ds_low[k0:k1, qs], kv[d, 0, k0:k1, :], TN, preferred_element_type=F32
-                )
             return carry
 
         lax.fori_loop(0, heads, body, 0)
         acc[into, 0] = acc[into, 0] * scale
+
+    def query_grads(hooks):
+        def body(h, carry):
+            run_hooks(h, hooks)
+            cols = pl.ds(pl.multiple_of(h * dh, dh), dh)
+            for qc in range(2):
+                qs = slice(qc * hb, (qc + 1) * hb)
+                total = 0.0
+                edge = (REACH * tok) if qc == 0 else (REACH * tok + hb)
+                spans = ((0, hb), (tok, blocks * tok)) if qc == 0 else ((0, REACH * tok), (edge, blocks * tok))
+                for r0, r1 in spans:
+                    total += lax.dot_general(
+                        ds_ref[h, r0:r1, qs].astype(BF16), kv[0, r0:r1, :], TN, preferred_element_type=F32
+                    )
+                dq_ref[qs, cols] = (total * scale).astype(BF16)
+            return carry
+
+        lax.fori_loop(0, heads, body, 0)
 
     def pair_out(d):
         @pl.when(s >= d)
         def _():
             pair_send[d] = acc[d % 2, 1 - c].astype(BF16)
 
-        send(s >= d, pair_send.at[d], pair_recv.at[d], pair_sem.at[d], mate)
+        send(lambda: s >= d, pair_send.at[d], pair_recv.at[d], pair_sem.at[d], mate)
 
     def half_out(d):
         @pl.when(s >= d)
@@ -283,7 +322,7 @@
             half_send[d] = (acc[d % 2, c, there, :] + pair_recv[d, there, :].astype(F32)).astype(BF16)
             half_keep[d] = acc[d % 2, c, here, :] + pair_recv[d, here, :].astype(F32)
 
-        send(s >= d, half_send.at[d], half_recv.at[d], half_sem.at[d], across)
+        send(lambda: s >= d, half_send.at[d], half_recv.at[d], half_sem.at[d], across)
 
     def quarter_out(d):
         @pl.when(s >= d)
@@ -296,21 +335,24 @@
                 own_quart[...] = mine
 
         if d:
-            send(s >= d, quart_send.at[d - 1], quart_recv.at[d - 1], quart_sem.at[d - 1], (s - d, hd))
-
+            send(lambda: s >= d, quart_send.at[d - 1], quart_recv.at[d - 1], quart_sem.at[d - 1], (s - d, hd))
+
+    plan = {
+        4: {},
+        3: {2: [lambda: half_out(4)]},
+        2: {2: [lambda: half_out(3)]},
+        1: {2: [lambda: half_out(2), lambda: quarter_out(4)]},
+        0: {2: [lambda: half_out(1), lambda: quarter_out(3)]},
+    }
     for d in range(REACH, -1, -1):
         @pl.when(s >= d)
         def _(d=d):
-            grads_of(d if d in (0, REACH) else s * 0 + d, d % 2)
+            grads_of(d, plan[d])
 
         pair_out(d)
-        if d + 1 <= REACH:
-            half_out(d + 1)
-        if d + 2 <= REACH:
-            quarter_out(d + 2)
-    for h in range(heads):
-        dq_out[:, h * dh : (h + 1) * dh] = (dq_acc[h] * scale).astype(BF16)
-    half_out(0)
+    query_grads({1: [lambda: half_out(0)], 2: [lambda: quarter_out(2)]})
+    write_dq = pltpu.make_async_copy(dq_ref, dq_out, load_sem.at[0])
+    write_dq.start()
     quarter_out(1)
     quarter_out(0)
     for d in range(REACH, 0, -1):
@@ -323,7 +365,7 @@
         return fin.at[array, half(index), :]
 
     fin[c, half(xh), :] = own_quart[...].astype(BF16)
-    always = s >= 0
+    always = lambda: s >= 0
     send(always, fin_half(c, xh), fin_half(c, xh), fin_sem.at[0], across)
     send(always, fin_half(c, xh), fin_half(c, xh), fin_sem.at[1], mate)
     arrived(fin_half(c, 1 - xh), fin_sem.at[0])
@@ -331,10 +373,8 @@
     arrived(fin_half(1 - c, xh), fin_sem.at[1])
     arrived(fin_half(1 - c, 1 - xh), fin_sem.at[2])
     fin_out[...] = fin[...]
-    for cond, copy in pending:
-        @pl.when(cond)
-        def _(copy=copy):
-            copy.wait_send()
+    write_dq.wait()
+    wait_sent()
 
 
 def on_device(query, key_rows, value_rows, grad_out):
@@ -350,19 +390,18 @@
             jax.ShapeDtypeStruct((2, tok, dh), BF16),
         ),
         in_specs=[pl.BlockSpec(memory_space=pl.ANY)] * 4,
-        out_specs=(pl.BlockSpec(memory_space=vmem),) * 2,
+        out_specs=(pl.BlockSpec(memory_space=pl.ANY), pl.BlockSpec(memory_space=vmem)),
         scratch_shapes=[
             vmem((tok, heads * dh), BF16),
             vmem((tok, heads * dh), BF16),
-            vmem((blocks, 2, tok, dh), BF16),
+            vmem((2, blocks * tok, dh), BF16),
             vmem((blocks, heads, tok, tok), F32),
-            vmem((blocks, heads, tok, tok), F32),
+            vmem((heads, blocks * tok, tok), F32),
             vmem((blocks, heads, 1, tok), F32),
             vmem((heads, 1, tok), F32),
             vmem((heads, 1, tok), F32),
             vmem((heads, 1, tok), F32),
-            vmem((tok, tok), BF16),
-            vmem((heads, tok, dh), F32),
+            vmem((tok, heads * dh), BF16),
             vmem((2, 2, tok, dh), F32),
             vmem((blocks, tok, dh), BF16),
             vmem((blocks, tok, dh), BF16),

time: 71.4 us -> 64.7 us (0.906)
  the two profiles are of different devices: /device:TPU:31 before, /device:TPU:25 now
where the time goes in v2:
time: 64.7 us; the launch traced here: 63.7 us
  Pallas kernels  59.9 us (93%)
  other arithmetic  2.16 us (3%)
  local copies, waits for them, and re-layouts  0.97 us (1%)
  between operations  0.65 us (1%)
    pallas_call x1, Pallas kernels, on_device(): pl.pallas_call(kernel, out_shape=(jax.ShapeDtypeStruct(query.shape, BF16)...  59.9 us
    convert_element_type x1, other arithmetic, on_device(): return (grad_query, fin[0].astype(F32), fin[1].astype(F32))  2.16 us

profile of v2, /device:TPU:25, one launch (start us, length us, event | category | flops | bytes accessed | tf_op | source)
XLA Modules:
  0.0 63.7 jit_solution(12684885140080274279)
XLA Ops:
  0.6 59.9 %shard_map.67 = (bf16[512,1024]{1,0:T(8,128)(2,1)}, bf16[2,512,256]{2,1,0:T(8,128)(2,1)}) custom-call(bf16[512,1024]{1,0:T(8,128)(2,1)} %q_hbm.1, bf16[512,1024]{1,0:T(8,128)(2,1)} %g_hbm.1, bf16[512,256]{1,0:T(8,128)(2,1)} %k_hbm.1, bf16[512,256]{1,0:T(8,128)(2,1)} %v_hbm.1), custom_call_target="tpu_custom_call" | custom-call | tf_op jit(solution)/shard_map/pallas_call | solution.py:386
  60.5 0.0 copy-start
  60.5 2.2 %bitcast_convert_fusion = (f32[512,256]{1,0:T(8,128)}, f32[512,256]{1,0:T(8,128)}) fusion(bf16[2,512,256]{2,1,0:T(8,128)(2,1)} %get-tuple-element.6), kind=kLoop, calls=%fused_computation | loop fusion | flops 262144 | bytes 1572864 | tf_op jit(solution)/shard_map/convert_element_type | solution.py:428
  62.7 0.0 copy-done
  62.7 1.0 %copy.8 = bf16[512,1024]{1,0:T(8,128)(2,1)} copy(bf16[512,1024]{1,0:T(8,128)(2,1)S(1)} %copy-done) | data formatting | bytes 2097152
Async XLA Ops:
  60.5 2.2 %copy-start = (bf16[512,1024]{1,0:T(8,128)(2,1)S(1)}, bf16[512,1024]{1,0:T(8,128)(2,1)}, u32[]{:S(2)}) copy-start(bf16[512,1024]{1,0:T(8,128)(2,1)} %get-tuple-element.12) | copy-start | bytes 3145732

commit v3 on v2

--- a/solution.py
+++ b/solution.py
@@ -68,7 +68,7 @@
     ahead = jnp.minimum(n_seq - 1 - s, REACH)
     behind = jnp.minimum(s, REACH)
     pl.semaphore_wait(barrier, 4 + ahead + behind)
-    for load in loads:
+    for load in loads[:2]:
         load.wait()
 
     pending = []
@@ -178,10 +178,9 @@
                 for step in steps:
                     step()
 
-    def scores_of(d, kind, hooks):
-        def body(h, carry):
-            run_hooks(h, hooks)
-            cols = pl.ds(pl.multiple_of(h * dh, dh), dh)
+    def scores_of(d, kind):
+        for h in range(heads):
+            cols = slice(h * dh, (h + 1) * dh)
             for qc in range(2):
                 k0, k1 = key_range(kind, qc)
                 rows = rows_of(d, k0, k1)
@@ -213,11 +212,10 @@
                 m_run[h, :, qs] = top
                 l_run[h, :, qs] = total
                 dl_run[h, :, qs] = dots
-            return carry
-
-        lax.fori_loop(0, heads, body, 0)
-
-    scores_of(0, 0, {})
+
+    for load in loads[2:]:
+        load.wait()
+    scores_of(0, 0)
     for d in range(1, REACH + 1):
         @pl.when(s < d)
         def _(d=d):
@@ -226,68 +224,66 @@
                 ds_ref[h, d * tok : (d + 1) * tok, :] = jnp.zeros((tok, tok), F32)
 
     relay_two(0)
+    relay_two(1, 0)
     relay_odd(lambda: xl == 1, 1)
-    odd_second = 1 + 2 * xl
-    late = (xl == 0) & (s >= 4)
-
-    @pl.when(xl == 1)
+    first, second = 2 - xl, 1 + xl
+
+    @pl.when(s >= first)
     def _():
-        mate_ready(1)
-        scores_of(1, 1, {2: [lambda: relay_two(1, 1)]})
-
-    relay_two(1, 0)
-
-    @pl.when(s >= 2)
+        mate_ready(first)
+        scores_of(first, 1)
+
+    relay_two(1, 1)
+    relay_odd(lambda: (xl == 0) & (s >= 1), 1)
+    relay_four(0)
+
+    @pl.when(s >= second)
     def _():
-        mate_ready(2)
-        scores_of(2, 2, {1: [lambda: relay_odd(lambda: s >= odd_second, odd_second)], 3: [lambda: relay_four(0)]})
-
-    @pl.when(s >= odd_second)
-    def _():
-        mate_ready(odd_second)
-        scores_of(odd_second, 1, {3: [lambda: relay_four(1)]})
+        mate_ready(second)
+        scores_of(second, 1)
+
+    relay_odd(lambda: (xl == 1) & (s >= 3), 3)
+    relay_four(1)
 
     @pl.when(s >= 4)
     def _():
         mate_ready(4)
-        scores_of(4, 4, {2: [lambda: relay_odd(lambda: (xl == 0) & (s >= 4), 3)]})
-
-    @pl.when(late)
+        scores_of(4, 4)
+
+    relay_odd(lambda: (xl == 0) & (s >= 3), 3)
+
+    @pl.when(s >= 3)
     def _():
         mate_ready(3)
-        scores_of(3, 3, {})
+        scores_of(3, 3)
 
     inverse = 1.0 / l_run[...]
     dl_run[...] = dl_run[...] * inverse
     l_run[...] = inverse
 
-    def grads_of(d, hooks):
+    def grads_of(d):
         into = d % 2
-        acc[into] = jnp.zeros_like(acc[into])
-
-        def body(h, carry):
-            run_hooks(h, hooks)
-            cols = pl.ds(pl.multiple_of(h * dh, dh), dh)
-            weight = jnp.exp2(md[d, h] - m_run[h]) * l_run[h]
-            delta = dl_run[h]
-            for kc in range(2):
-                q0, q1 = query_range(d, kc)
-                ks, qs = slice(kc * hb, (kc + 1) * hb), slice(q0, q1)
-                rows = slice(d * tok + kc * hb, d * tok + (kc + 1) * hb)
-                probs = e_ref[d, h, ks, qs] * weight[:, q0:q1]
-                dscores = probs * (ds_ref[h, rows, qs] - delta[:, q0:q1])
-                probs_low, dscores_low = probs.astype(BF16), dscores.astype(BF16)
+        for kc in range(2):
+            q0, q1 = query_range(d, kc)
+            ks, qs = slice(kc * hb, (kc + 1) * hb), slice(q0, q1)
+            rows = slice(d * tok + kc * hb, d * tok + (kc + 1) * hb)
+            for h in range(heads):
+                cols = slice(h * dh, (h + 1) * dh)
+                weight = jnp.exp2(md[d, h, :, qs] - m_run[h, :, qs]) * l_run[h, :, qs]
+                probs = e_ref[d, h, ks, qs] * weight
+                dscores = probs * (ds_ref[h, rows, qs] - dl_run[h, :, qs])
                 ds_ref[h, rows, qs] = dscores
-                acc[into, 1, ks, :] += lax.dot_general(
-                    probs_low, g_ref[qs, cols], NN, preferred_element_type=F32
+                to_value = lax.dot_general(
+                    probs.astype(BF16), g_ref[qs, cols], NN, preferred_element_type=F32
                 )
-                acc[into, 0, ks, :] += lax.dot_general(
-                    dscores_low, q_ref[qs, cols], NN, preferred_element_type=F32
+                to_key = lax.dot_general(
+                    dscores.astype(BF16), q_ref[qs, cols], NN, preferred_element_type=F32
                 )
-            return carry
-
-        lax.fori_loop(0, heads, body, 0)
-        acc[into, 0] = acc[into, 0] * scale
+                if h:
+                    to_value += acc[into, 1, ks, :]
+                    to_key += acc[into, 0, ks, :]
+                acc[into, 1, ks, :] = to_value
+                acc[into, 0, ks, :] = to_key * scale if h == heads - 1 else to_key
 
     def query_grads(hooks):
         def body(h, carry):
@@ -337,20 +333,16 @@
         if d:
             send(lambda: s >= d, quart_send.at[d - 1], quart_recv.at[d - 1], quart_sem.at[d - 1], (s - d, hd))
 
-    plan = {
-        4: {},
-        3: {2: [lambda: half_out(4)]},
-        2: {2: [lambda: half_out(3)]},
-        1: {2: [lambda: half_out(2), lambda: quarter_out(4)]},
-        0: {2: [lambda: half_out(1), lambda: quarter_out(3)]},
-    }
     for d in range(REACH, -1, -1):
         @pl.when(s >= d)
         def _(d=d):
-            grads_of(d, plan[d])
+            grads_of(d)
 
         pair_out(d)
-    query_grads({1: [lambda: half_out(0)], 2: [lambda: quarter_out(2)]})
+        if d < REACH:
+            half_out(d + 1)
+    half_out(0)
+    query_grads({0: [lambda: quarter_out(4)], 1: [lambda: quarter_out(3)], 3: [lambda: quarter_out(2)]})
     write_dq = pltpu.make_async_copy(dq_ref, dq_out, load_sem.at[0])
     write_dq.start()
     quarter_out(1)
@@ -372,9 +364,36 @@
     send(always, fin_half(c, 1 - xh), fin_half(c, 1 - xh), fin_sem.at[2], mate)
     arrived(fin_half(1 - c, xh), fin_sem.at[1])
     arrived(fin_half(1 - c, 1 - xh), fin_sem.at[2])
-    fin_out[...] = fin[...]
+    write_fin = pltpu.make_async_copy(fin, fin_out, load_sem.at[1])
+    write_fin.start()
+    write_fin.wait()
     write_dq.wait()
     wait_sent()
+
+
+def finish(dq_hbm, fin_hbm, dq_out, dk_out, dv_out, dq_buf, fin_buf, wide, in_sem, out_sem):
+    parts = dq_buf.shape[0]
+    rows = dq_buf.shape[1]
+    fin_in = pltpu.make_async_copy(fin_hbm, fin_buf, in_sem.at[parts])
+    fin_in.start()
+
+    def span(i):
+        return slice(i * rows, (i + 1) * rows)
+
+    loads = [pltpu.make_async_copy(dq_hbm.at[span(i)], dq_buf.at[i], in_sem.at[i]) for i in range(parts)]
+    stores = [pltpu.make_async_copy(dq_buf.at[i], dq_out.at[span(i)], out_sem.at[i]) for i in range(parts)]
+    for load in loads:
+        load.start()
+    fin_in.wait()
+    for array, out in enumerate((dk_out, dv_out)):
+        wide[array] = fin_buf[array].astype(F32)
+        stores.append(pltpu.make_async_copy(wide.at[array], out, out_sem.at[parts + array]))
+        stores[-1].start()
+    for load, store in zip(loads, stores):
+        load.wait()
+        store.start()
+    for store in stores:
+        store.wait()
 
 
 def on_device(query, key_rows, value_rows, grad_out):
@@ -390,7 +409,7 @@
             jax.ShapeDtypeStruct((2, tok, dh), BF16),
         ),
         in_specs=[pl.BlockSpec(memory_space=pl.ANY)] * 4,
-        out_specs=(pl.BlockSpec(memory_space=pl.ANY), pl.BlockSpec(memory_space=vmem)),
+        out_specs=(pl.BlockSpec(memory_space=pl.ANY),) * 2,
         scratch_shapes=[
             vmem((tok, heads * dh), BF16),
             vmem((tok, heads * dh), BF16),
@@ -425,7 +444,25 @@
             collective_id=0, has_side_effects=True, vmem_limit_bytes=67043328
         ),
     )(query, grad_out, key_rows, value_rows)
-    return grad_query, fin[0].astype(F32), fin[1].astype(F32)
+    parts = 4
+    anywhere = pl.BlockSpec(memory_space=pl.ANY)
+    return pl.pallas_call(
+        finish,
+        out_shape=(
+            jax.ShapeDtypeStruct(query.shape, BF16),
+            jax.ShapeDtypeStruct((tok, dh), F32),
+            jax.ShapeDtypeStruct((tok, dh), F32),
+        ),
+        in_specs=[anywhere] * 2,
+        out_specs=(anywhere,) * 3,
+        scratch_shapes=[
+            vmem((parts, tok // parts, heads * dh), BF16),
+            vmem((2, tok, dh), BF16),
+            vmem((2, tok, dh), F32),
+            dma((parts + 1,)),
+            dma((parts + 2,)),
+        ],
+    )(grad_query, fin)
 
 
 def solution(mesh):

time: 64.7 us -> 62.8 us (0.971)
  the two profiles are of different devices: /device:TPU:25 before, /device:TPU:19 now
where the time goes in v3:
time: 62.8 us; the launch traced here: 62.6 us
  Pallas kernels  61.8 us (98%)
  between operations  0.8 us (1%)
    pallas_call x1, Pallas kernels, on_device(): pl.pallas_call(kernel, out_shape=(jax.ShapeDtypeStruct(query.shape, BF16)...  59.4 us
    pallas_call x1, Pallas kernels, on_device(): pl.pallas_call(finish, out_shape=(jax.ShapeDtypeStruct(query.shape, BF16)...  2.48 us

profile of v3, /device:TPU:19, one launch (start us, length us, event | category | flops | bytes accessed | tf_op | source)
XLA Modules:
  0.0 62.6 jit_solution(6273986750003773802)
XLA Ops:
  0.6 59.4 %shard_map.67 = (bf16[512,1024]{1,0:T(8,128)(2,1)}, bf16[2,512,256]{2,1,0:T(8,128)(2,1)}) custom-call(bf16[512,1024]{1,0:T(8,128)(2,1)} %q_hbm.1, bf16[512,1024]{1,0:T(8,128)(2,1)} %g_hbm.1, bf16[512,256]{1,0:T(8,128)(2,1)} %k_hbm.1, bf16[512,256]{1,0:T(8,128)(2,1)} %v_hbm.1), custom_call_target="tpu_custom_call" | custom-call | tf_op jit(solution)/shard_map/pallas_call | solution.py:405
  60.0 2.5 %shard_map.68 = (bf16[512,1024]{1,0:T(8,128)(2,1)}, f32[512,256]{1,0:T(8,128)}, f32[512,256]{1,0:T(8,128)}) custom-call(bf16[512,1024]{1,0:T(8,128)(2,1)} %get-tuple-element.5.dq_hbm, bf16[2,512,256]{2,1,0:T(8,128)(2,1)} %get-tuple-element.6.fin_hbm), custom_call_target="tpu_custom_call" | custom-call | tf_op jit(solution)/shard_map/pallas_call | solution.py:449

commit v4 on v3

--- a/solution.py
+++ b/solution.py
@@ -20,9 +20,9 @@
     q_hbm, g_hbm, k_hbm, v_hbm,
     dq_out, fin_out,
     q_ref, g_ref, kv, e_ref, ds_ref, md, m_run, l_run, dl_run, dq_ref,
-    acc, pair_send, pair_recv, half_keep, half_send, half_recv,
-    quart_send, quart_recv, own_quart, fin,
-    load_sem, send_sem, net_sem, mate_sem, pair_sem, half_sem, quart_sem, fin_sem,
+    acc, pair_send, pair_recv, keep, odd_send, opp_recv, chain_send, chain_recv,
+    fin_send, fin_recv, fin,
+    load_sem, send_sem, net_sem, mate_sem, pair_sem, opp_sem, chain_sem, across_sem, fin_sem,
 ):
     tok, dh = e_ref.shape[2], kv.shape[2]
     heads = e_ref.shape[1]
@@ -57,17 +57,16 @@
         greet((opp, head))
     greet(mate)
     greet(across)
-    for d in range(1, REACH + 1):
-        @pl.when(s + d < n_seq)
-        def _(d=d):
-            greet((s + d, hd))
-
-        @pl.when(s >= d)
-        def _(d=d):
-            greet((s - d, hd))
-    ahead = jnp.minimum(n_seq - 1 - s, REACH)
-    behind = jnp.minimum(s, REACH)
-    pl.semaphore_wait(barrier, 4 + ahead + behind)
+
+    @pl.when(s + 2 < n_seq)
+    def _():
+        greet((s + 2, hd))
+
+    @pl.when(s >= 2)
+    def _():
+        greet((s - 2, hd))
+
+    pl.semaphore_wait(barrier, 4 + jnp.minimum(n_seq - 1 - s, 2) // 2 + jnp.minimum(s, 2) // 2)
     for load in loads[:2]:
         load.wait()
 
@@ -261,8 +260,7 @@
     dl_run[...] = dl_run[...] * inverse
     l_run[...] = inverse
 
-    def grads_of(d):
-        into = d % 2
+    def grads_of(d, into):
         for kc in range(2):
             q0, q1 = query_range(d, kc)
             ks, qs = slice(kc * hb, (kc + 1) * hb), slice(q0, q1)
@@ -306,64 +304,102 @@
     def pair_out(d):
         @pl.when(s >= d)
         def _():
-            pair_send[d] = acc[d % 2, 1 - c].astype(BF16)
+            pair_send[d] = acc[place[d], 1 - c].astype(BF16)
 
         send(lambda: s >= d, pair_send.at[d], pair_recv.at[d], pair_sem.at[d], mate)
 
-    def half_out(d):
+    def odd_out(d):
+        o = d // 2
+
         @pl.when(s >= d)
         def _():
             arrived(pair_recv.at[d], pair_sem.at[d])
-            there, here = half(1 - xh), half(xh)
-            half_send[d] = (acc[d % 2, c, there, :] + pair_recv[d, there, :].astype(F32)).astype(BF16)
-            half_keep[d] = acc[d % 2, c, here, :] + pair_recv[d, here, :].astype(F32)
-
-        send(lambda: s >= d, half_send.at[d], half_recv.at[d], half_sem.at[d], across)
-
-    def quarter_out(d):
+            odd_send[o] = (acc[place[d], c] + pair_recv[d].astype(F32)).astype(BF16)
+
+        for x_hi in range(2):
+            send(
+                lambda: s >= d, odd_send.at[o, x_hi * hb : (x_hi + 1) * hb], opp_recv.at[o, xh],
+                opp_sem.at[o, xh], (opp, 2 * x_hi + c),
+            )
+
+    def base(d):
         @pl.when(s >= d)
         def _():
-            arrived(half_recv.at[d], half_sem.at[d])
-            mine = half_keep[d] + half_recv[d].astype(F32)
-            if d:
-                quart_send[d - 1] = mine.astype(BF16)
-            else:
-                own_quart[...] = mine
-
-        if d:
-            send(lambda: s >= d, quart_send.at[d - 1], quart_recv.at[d - 1], quart_sem.at[d - 1], (s - d, hd))
-
-    for d in range(REACH, -1, -1):
+            arrived(pair_recv.at[d], pair_sem.at[d])
+            keep[d // 2] = acc[place[d], c] + pair_recv[d].astype(F32)
+
+    def add_opp(o):
+        @pl.when(s >= 2 * o + 2 * xl)
+        def _():
+            for x_hi in range(2):
+                arrived(opp_recv.at[o, x_hi], opp_sem.at[o, x_hi])
+            keep[o + xl, half(xh), :] += opp_recv[o, 0].astype(F32) + opp_recv[o, 1].astype(F32)
+
+    def add_chain(i, index):
+        @pl.when((s >= 2 - 2 * i) & (s + 2 < n_seq))
+        def _():
+            arrived(chain_recv.at[i, half(index), :], chain_sem.at[i, index])
+            keep[1 - i, half(index), :] += chain_recv[i, half(index), :].astype(F32)
+
+    def chain_out(i, index, parity=None):
+        def here():
+            some = s >= 4 - 2 * i
+            return some if parity is None else some & (xl == parity)
+
+        @pl.when(here())
+        def _():
+            chain_send[i, half(index), :] = keep[2 - i, half(index), :].astype(BF16)
+
+        send(
+            here, chain_send.at[i, half(index), :], chain_recv.at[i, half(index), :],
+            chain_sem.at[i, index], (s - 2, hd),
+        )
+
+    def first_chain():
+        base(4)
+        chain_out(0, 1 - xh)
+        chain_out(0, xh, 0)
+
+    def second_base():
+        base(2)
+
+    def last_of_four():
+        add_opp(1)
+        chain_out(0, xh, 1)
+
+    def early_two():
+        add_chain(0, 1 - xh)
+        chain_out(1, 1 - xh)
+
+    steps = ((3, None), (4, lambda: odd_out(3)), (1, first_chain), (2, lambda: odd_out(1)), (0, second_base))
+    place = {d: i % 2 for i, (d, _) in enumerate(steps)}
+    for d, after in steps:
         @pl.when(s >= d)
         def _(d=d):
-            grads_of(d)
+            grads_of(d, place[d])
 
         pair_out(d)
-        if d < REACH:
-            half_out(d + 1)
-    half_out(0)
-    query_grads({0: [lambda: quarter_out(4)], 1: [lambda: quarter_out(3)], 3: [lambda: quarter_out(2)]})
+        if after is not None:
+            after()
+    query_grads({0: [last_of_four], 1: [lambda: base(0)], 2: [early_two]})
     write_dq = pltpu.make_async_copy(dq_ref, dq_out, load_sem.at[0])
     write_dq.start()
-    quarter_out(1)
-    quarter_out(0)
-    for d in range(REACH, 0, -1):
-        @pl.when(s + d < n_seq)
-        def _(d=d):
-            arrived(quart_recv.at[d - 1], quart_sem.at[d - 1])
-            own_quart[...] += quart_recv[d - 1].astype(F32)
-
-    def fin_half(array, index):
-        return fin.at[array, half(index), :]
-
-    fin[c, half(xh), :] = own_quart[...].astype(BF16)
+    add_opp(0)
+    add_chain(0, xh)
+    chain_out(1, xh)
     always = lambda: s >= 0
-    send(always, fin_half(c, xh), fin_half(c, xh), fin_sem.at[0], across)
-    send(always, fin_half(c, xh), fin_half(c, xh), fin_sem.at[1], mate)
-    arrived(fin_half(c, 1 - xh), fin_sem.at[0])
-    send(always, fin_half(c, 1 - xh), fin_half(c, 1 - xh), fin_sem.at[2], mate)
-    arrived(fin_half(1 - c, xh), fin_sem.at[1])
-    arrived(fin_half(1 - c, 1 - xh), fin_sem.at[2])
+    for index in (1 - xh, xh):
+        rows = half(index)
+        add_chain(1, index)
+        fin_send[rows, :] = keep[0, rows, :].astype(BF16)
+        send(always, fin_send.at[rows, :], fin_recv.at[rows, :], across_sem.at[index], across)
+    for index in (xh, 1 - xh):
+        rows = half(index)
+        arrived(fin_recv.at[rows, :], across_sem.at[index])
+        fin[c, rows, :] = (fin_send[rows, :].astype(F32) + fin_recv[rows, :].astype(F32)).astype(BF16)
+        send(always, fin.at[c, rows, :], fin.at[c, rows, :], fin_sem.at[index], mate)
+    for index in (xh, 1 - xh):
+        arrived(fin.at[1 - c, half(index), :], fin_sem.at[index])
     write_fin = pltpu.make_async_copy(fin, fin_out, load_sem.at[1])
     write_fin.start()
     write_fin.wait()
@@ -424,21 +460,23 @@
             vmem((2, 2, tok, dh), F32),
             vmem((blocks, tok, dh), BF16),
             vmem((blocks, tok, dh), BF16),
-            vmem((blocks, tok // 2, dh), F32),
-            vmem((blocks, tok // 2, dh), BF16),
-            vmem((blocks, tok // 2, dh), BF16),
-            vmem((REACH, tok // 2, dh), BF16),
-            vmem((REACH, tok // 2, dh), BF16),
-            vmem((tok // 2, dh), F32),
+            vmem((3, tok, dh), F32),
+            vmem((2, tok, dh), BF16),
+            vmem((2, 2, tok // 2, dh), BF16),
+            vmem((2, tok, dh), BF16),
+            vmem((2, tok, dh), BF16),
+            vmem((tok, dh), BF16),
+            vmem((tok, dh), BF16),
             vmem((2, tok, dh), BF16),
             dma((4,)),
             dma((64,)),
             dma((blocks, 2)),
             dma((blocks, 2)),
             dma((blocks,)),
-            dma((blocks,)),
-            dma((REACH,)),
-            dma((3,)),
+            dma((2, 2)),
+            dma((2, 2)),
+            dma((2,)),
+            dma((2,)),
         ],
         compiler_params=pltpu.CompilerParams(
             collective_id=0, has_side_effects=True, vmem_limit_bytes=67043328

time: 62.8 us -> 56.4 us (0.90)
  the two profiles are of different devices: /device:TPU:19 before, /device:TPU:25 now
where the time goes in v4:
time: 56.4 us; the launch traced here: 56.3 us
  Pallas kernels  55.5 us (98%)
  between operations  0.8 us (1%)
    pallas_call x1, Pallas kernels, on_device(): pl.pallas_call(kernel, out_shape=(jax.ShapeDtypeStruct(query.shape, BF16)...  53 us
    pallas_call x1, Pallas kernels, on_device(): pl.pallas_call(finish, out_shape=(jax.ShapeDtypeStruct(query.shape, BF16)...  2.48 us

profile of v4, /device:TPU:25, one launch (start us, length us, event | category | flops | bytes accessed | tf_op | source)
XLA Modules:
  0.0 56.3 jit_solution(5800050010260725629)
XLA Ops:
  0.6 53.0 %shard_map.67 = (bf16[512,1024]{1,0:T(8,128)(2,1)}, bf16[2,512,256]{2,1,0:T(8,128)(2,1)}) custom-call(bf16[512,1024]{1,0:T(8,128)(2,1)} %q_hbm.1, bf16[512,1024]{1,0:T(8,128)(2,1)} %g_hbm.1, bf16[512,256]{1,0:T(8,128)(2,1)} %k_hbm.1, bf16[512,256]{1,0:T(8,128)(2,1)} %v_hbm.1), custom_call_target="tpu_custom_call" | custom-call | tf_op jit(solution)/shard_map/pallas_call | solution.py:441
  53.6 2.5 %shard_map.68 = (bf16[512,1024]{1,0:T(8,128)(2,1)}, f32[512,256]{1,0:T(8,128)}, f32[512,256]{1,0:T(8,128)}) custom-call(bf16[512,1024]{1,0:T(8,128)(2,1)} %get-tuple-element.5.dq_hbm, bf16[2,512,256]{2,1,0:T(8,128)(2,1)} %get-tuple-element.6.fin_hbm), custom_call_target="tpu_custom_call" | custom-call | tf_op jit(solution)/shard_map/pallas_call | solution.py:487

commit v5 on v4

--- a/solution.py
+++ b/solution.py
@@ -9,6 +9,7 @@
 BF16 = jnp.bfloat16
 MESH = pl.DeviceIdType.MESH
 REACH = 4
+PIECES = 2
 LOG2E = 1.4426950408889634
 NEG = -1e30
 NT = (((1,), (1,)), ((), ()))
@@ -18,15 +19,16 @@
 
 def kernel(
     q_hbm, g_hbm, k_hbm, v_hbm,
-    dq_out, fin_out,
-    q_ref, g_ref, kv, e_ref, ds_ref, md, m_run, l_run, dl_run, dq_ref,
+    dq_ref, fin,
+    q_ref, g_ref, kv, e_ref, ds_ref, md, m_run, l_run, dl_run,
     acc, pair_send, pair_recv, keep, odd_send, opp_recv, chain_send, chain_recv,
-    fin_send, fin_recv, fin,
+    fin_send, fin_recv,
     load_sem, send_sem, net_sem, mate_sem, pair_sem, opp_sem, chain_sem, across_sem, fin_sem,
 ):
     tok, dh = e_ref.shape[2], kv.shape[2]
     heads = e_ref.shape[1]
     hb = tok // 2
+    sb = hb // PIECES
     blocks = REACH + 1
     scale = dh ** (-0.5)
     to_log2 = scale * LOG2E
@@ -37,8 +39,8 @@
     mate = (s, hd + 1 - 2 * c)
     across = (s, lax.rem(hd + 2, 4))
 
-    def half(index):
-        return pl.ds(pl.multiple_of(index * hb, hb), hb)
+    def piece(index, sub):
+        return pl.ds(pl.multiple_of(index * hb + sub * sb, sb), sb)
 
     loads = [
         pltpu.make_async_copy(src, dst, load_sem.at[i])
@@ -107,11 +109,14 @@
     def kv_half(d, array, index):
         return kv.at[array, pl.ds(pl.multiple_of(d * tok + index * hb, hb), hb), :]
 
-    def over_x(cond, src_slot, dst_slot):
+    def kv_piece(d, array, index, sub):
+        return kv.at[array, pl.ds(pl.multiple_of(d * tok + index * hb + sub * sb, sb), sb), :]
+
+    def over_x(cond, src_slot, dst_slot, sub):
         for x_hi in range(2):
             send(
-                cond, kv_half(src_slot, c, xh), kv_half(dst_slot, c, xh), net_sem.at[dst_slot, xh],
-                (opp, 2 * x_hi + c),
+                cond, kv_piece(src_slot, c, xh, sub), kv_piece(dst_slot, c, xh, sub),
+                net_sem.at[dst_slot, xh, sub], (opp, 2 * x_hi + c),
             )
 
     def to_mate(cond, d, index):
@@ -119,34 +124,44 @@
 
     order = (xh, 1 - xh)
     for index in order:
-        send(lambda: s + 2 < n_seq, kv_half(0, c, index), kv_half(2, c, index), net_sem.at[2, index], (s + 2, hd))
-        if index is order[0]:
-            over_x(lambda: xl == 0, 0, 1)
+        for sub in range(PIECES):
+            send(
+                lambda: s + 2 < n_seq, kv_piece(0, c, index, sub), kv_piece(2, c, index, sub),
+                net_sem.at[2, index, sub], (s + 2, hd),
+            )
+            if index is order[0]:
+                over_x(lambda: xl == 0, 0, 1, sub)
 
     def relay_two(j, parity=None):
         def here():
             return (s >= 2) if parity is None else (s >= 2) & (xl == parity)
 
         index = order[j]
-        when_arrived(here, kv_half(2, c, index), net_sem.at[2, index])
-        send(
-            lambda: here() & (s + 2 < n_seq), kv_half(2, c, index), kv_half(4, c, index),
-            net_sem.at[4, index], (s + 2, hd),
-        )
-        if j == 0:
-            over_x(here, 2, 3 - 2 * xl)
+        for sub in range(PIECES):
+            when_arrived(here, kv_piece(2, c, index, sub), net_sem.at[2, index, sub])
+            send(
+                lambda: here() & (s + 2 < n_seq), kv_piece(2, c, index, sub), kv_piece(4, c, index, sub),
+                net_sem.at[4, index, sub], (s + 2, hd),
+            )
+            if j == 0:
+                over_x(here, 2, 3 - 2 * xl, sub)
         to_mate(here, 2, index)
 
-    def relay_four(j):
+    def relay_four(j, parity=None):
+        def here():
+            return (s >= 4) if parity is None else (s >= 4) & (xl == parity)
+
         index = order[j]
-        when_arrived(lambda: s >= 4, kv_half(4, c, index), net_sem.at[4, index])
-        if j == 0:
-            over_x(lambda: (s >= 4) & (xl == 1), 4, 3)
-        to_mate(lambda: s >= 4, 4, index)
+        for sub in range(PIECES):
+            when_arrived(here, kv_piece(4, c, index, sub), net_sem.at[4, index, sub])
+            if j == 0:
+                over_x(lambda: here() & (xl == 1), 4, 3, sub)
+        to_mate(here, 4, index)
 
     def relay_odd(cond, d):
         for index in range(2):
-            when_arrived(cond, kv_half(d, c, index), net_sem.at[d, index])
+            for sub in range(PIECES):
+                when_arrived(cond, kv_piece(d, c, index, sub), net_sem.at[d, index, sub])
             to_mate(cond, d, index)
 
     def mate_ready(d):
@@ -234,22 +249,22 @@
 
     relay_two(1, 1)
     relay_odd(lambda: (xl == 0) & (s >= 1), 1)
-    relay_four(0)
+    relay_four(0, 0)
 
     @pl.when(s >= second)
     def _():
         mate_ready(second)
         scores_of(second, 1)
 
+    relay_four(0, 1)
     relay_odd(lambda: (xl == 1) & (s >= 3), 3)
     relay_four(1)
+    relay_odd(lambda: (xl == 0) & (s >= 3), 3)
 
     @pl.when(s >= 4)
     def _():
         mate_ready(4)
         scores_of(4, 4)
-
-    relay_odd(lambda: (xl == 0) & (s >= 3), 3)
 
     @pl.when(s >= 3)
     def _():
@@ -316,11 +331,13 @@
             arrived(pair_recv.at[d], pair_sem.at[d])
             odd_send[o] = (acc[place[d], c] + pair_recv[d].astype(F32)).astype(BF16)
 
-        for x_hi in range(2):
-            send(
-                lambda: s >= d, odd_send.at[o, x_hi * hb : (x_hi + 1) * hb], opp_recv.at[o, xh],
-                opp_sem.at[o, xh], (opp, 2 * x_hi + c),
-            )
+        for sub in range(PIECES):
+            for x_hi in range(2):
+                r0 = x_hi * hb + sub * sb
+                send(
+                    lambda: s >= d, odd_send.at[o, r0 : r0 + sb], opp_recv.at[o, xh, sub],
+                    opp_sem.at[o, xh, sub], (opp, 2 * x_hi + c),
+                )
 
     def base(d):
         @pl.when(s >= d)
@@ -328,48 +345,55 @@
             arrived(pair_recv.at[d], pair_sem.at[d])
             keep[d // 2] = acc[place[d], c] + pair_recv[d].astype(F32)
 
-    def add_opp(o):
+    def add_opp(o, sub):
         @pl.when(s >= 2 * o + 2 * xl)
         def _():
             for x_hi in range(2):
-                arrived(opp_recv.at[o, x_hi], opp_sem.at[o, x_hi])
-            keep[o + xl, half(xh), :] += opp_recv[o, 0].astype(F32) + opp_recv[o, 1].astype(F32)
-
-    def add_chain(i, index):
+                arrived(opp_recv.at[o, x_hi, sub], opp_sem.at[o, x_hi, sub])
+            keep[o + xl, piece(xh, sub), :] += opp_recv[o, 0, sub].astype(F32) + opp_recv[o, 1, sub].astype(F32)
+
+    def add_chain(i, index, sub):
         @pl.when((s >= 2 - 2 * i) & (s + 2 < n_seq))
         def _():
-            arrived(chain_recv.at[i, half(index), :], chain_sem.at[i, index])
-            keep[1 - i, half(index), :] += chain_recv[i, half(index), :].astype(F32)
-
-    def chain_out(i, index, parity=None):
+            rows = piece(index, sub)
+            arrived(chain_recv.at[i, rows, :], chain_sem.at[i, index, sub])
+            keep[1 - i, rows, :] += chain_recv[i, rows, :].astype(F32)
+
+    def chain_out(i, index, sub, parity=None):
         def here():
             some = s >= 4 - 2 * i
             return some if parity is None else some & (xl == parity)
 
+        rows = piece(index, sub)
+
         @pl.when(here())
         def _():
-            chain_send[i, half(index), :] = keep[2 - i, half(index), :].astype(BF16)
+            chain_send[i, rows, :] = keep[2 - i, rows, :].astype(BF16)
 
         send(
-            here, chain_send.at[i, half(index), :], chain_recv.at[i, half(index), :],
-            chain_sem.at[i, index], (s - 2, hd),
+            here, chain_send.at[i, rows, :], chain_recv.at[i, rows, :], chain_sem.at[i, index, sub],
+            (s - 2, hd),
         )
 
     def first_chain():
         base(4)
-        chain_out(0, 1 - xh)
-        chain_out(0, xh, 0)
+        for sub in range(PIECES):
+            chain_out(0, 1 - xh, sub)
+        for sub in range(PIECES):
+            chain_out(0, xh, sub, 0)
 
     def second_base():
         base(2)
 
     def last_of_four():
-        add_opp(1)
-        chain_out(0, xh, 1)
+        for sub in range(PIECES):
+            add_opp(1, sub)
+            chain_out(0, xh, sub, 1)
 
     def early_two():
-        add_chain(0, 1 - xh)
-        chain_out(1, 1 - xh)
+        for sub in range(PIECES):
+            add_chain(0, 1 - xh, sub)
+            chain_out(1, 1 - xh, sub)
 
     steps = ((3, None), (4, lambda: odd_out(3)), (1, first_chain), (2, lambda: odd_out(1)), (0, second_base))
     place = {d: i % 2 for i, (d, _) in enumerate(steps)}
@@ -382,52 +406,36 @@
         if after is not None:
             after()
     query_grads({0: [last_of_four], 1: [lambda: base(0)], 2: [early_two]})
-    write_dq = pltpu.make_async_copy(dq_ref, dq_out, load_sem.at[0])
-    write_dq.start()
-    add_opp(0)
-    add_chain(0, xh)
-    chain_out(1, xh)
+    for sub in range(PIECES):
+        add_opp(0, sub)
+        add_chain(0, xh, sub)
+        chain_out(1, xh, sub)
     always = lambda: s >= 0
     for index in (1 - xh, xh):
-        rows = half(index)
-        add_chain(1, index)
-        fin_send[rows, :] = keep[0, rows, :].astype(BF16)
-        send(always, fin_send.at[rows, :], fin_recv.at[rows, :], across_sem.at[index], across)
+        for sub in range(PIECES):
+            rows = piece(index, sub)
+            add_chain(1, index, sub)
+            fin_send[rows, :] = keep[0, rows, :].astype(BF16)
+            send(always, fin_send.at[rows, :], fin_recv.at[rows, :], across_sem.at[index, sub], across)
     for index in (xh, 1 - xh):
-        rows = half(index)
-        arrived(fin_recv.at[rows, :], across_sem.at[index])
-        fin[c, rows, :] = (fin_send[rows, :].astype(F32) + fin_recv[rows, :].astype(F32)).astype(BF16)
-        send(always, fin.at[c, rows, :], fin.at[c, rows, :], fin_sem.at[index], mate)
+        for sub in range(PIECES):
+            rows = piece(index, sub)
+            arrived(fin_recv.at[rows, :], across_sem.at[index, sub])
+            fin[c, rows, :] = (fin_send[rows, :].astype(F32) + fin_recv[rows, :].astype(F32)).astype(BF16)
+            send(always, fin.at[c, rows, :], fin.at[c, rows, :], fin_sem.at[index, sub], mate)
     for index in (xh, 1 - xh):
-        arrived(fin.at[1 - c, half(index), :], fin_sem.at[index])
-    write_fin = pltpu.make_async_copy(fin, fin_out, load_sem.at[1])
-    write_fin.start()
-    write_fin.wait()
-    write_dq.wait()
+        for sub in range(PIECES):
+            arrived(fin.at[1 - c, piece(index, sub), :], fin_sem.at[index, sub])
     wait_sent()
 
 
-def finish(dq_hbm, fin_hbm, dq_out, dk_out, dv_out, dq_buf, fin_buf, wide, in_sem, out_sem):
-    parts = dq_buf.shape[0]
-    rows = dq_buf.shape[1]
-    fin_in = pltpu.make_async_copy(fin_hbm, fin_buf, in_sem.at[parts])
-    fin_in.start()
-
-    def span(i):
-        return slice(i * rows, (i + 1) * rows)
-
-    loads = [pltpu.make_async_copy(dq_hbm.at[span(i)], dq_buf.at[i], in_sem.at[i]) for i in range(parts)]
-    stores = [pltpu.make_async_copy(dq_buf.at[i], dq_out.at[span(i)], out_sem.at[i]) for i in range(parts)]
-    for load in loads:
-        load.start()
-    fin_in.wait()
+def finish(dq_in, fin_in, dq_out, dk_out, dv_out, wide, sem):
+    stores = [pltpu.make_async_copy(dq_in, dq_out, sem.at[2])]
+    stores[0].start()
     for array, out in enumerate((dk_out, dv_out)):
-        wide[array] = fin_buf[array].astype(F32)
-        stores.append(pltpu.make_async_copy(wide.at[array], out, out_sem.at[parts + array]))
+        wide[array] = fin_in[array].astype(F32)
+        stores.append(pltpu.make_async_copy(wide.at[array], out, sem.at[array]))
         stores[-1].start()
-    for load, store in zip(loads, stores):
-        load.wait()
-        store.start()
     for store in stores:
         store.wait()
 
@@ -441,11 +449,11 @@
     grad_query, fin = pl.pallas_call(
         kernel,
         out_shape=(
-            jax.ShapeDtypeStruct(query.shape, BF16),
-            jax.ShapeDtypeStruct((2, tok, dh), BF16),
+            vmem(query.shape, BF16),
+            vmem((2, tok, dh), BF16),
         ),
         in_specs=[pl.BlockSpec(memory_space=pl.ANY)] * 4,
-        out_specs=(pl.BlockSpec(memory_space=pl.ANY),) * 2,
+        out_specs=(pl.BlockSpec(memory_space=vmem),) * 2,
         scratch_shapes=[
             vmem((tok, heads * dh), BF16),
             vmem((tok, heads * dh), BF16),
@@ -456,33 +464,30 @@
             vmem((heads, 1, tok), F32),
             vmem((heads, 1, tok), F32),
             vmem((heads, 1, tok), F32),
-            vmem((tok, heads * dh), BF16),
             vmem((2, 2, tok, dh), F32),
             vmem((blocks, tok, dh), BF16),
             vmem((blocks, tok, dh), BF16),
             vmem((3, tok, dh), F32),
             vmem((2, tok, dh), BF16),
-            vmem((2, 2, tok // 2, dh), BF16),
+            vmem((2, 2, PIECES, tok // 2 // PIECES, dh), BF16),
             vmem((2, tok, dh), BF16),
             vmem((2, tok, dh), BF16),
             vmem((tok, dh), BF16),
             vmem((tok, dh), BF16),
-            vmem((2, tok, dh), BF16),
             dma((4,)),
-            dma((64,)),
-            dma((blocks, 2)),
+            dma((128,)),
+            dma((blocks, 2, PIECES)),
             dma((blocks, 2)),
             dma((blocks,)),
-            dma((2, 2)),
-            dma((2, 2)),
-            dma((2,)),
-            dma((2,)),
+            dma((2, 2, PIECES)),
+            dma((2, 2, PIECES)),
+            dma((2, PIECES)),
+            dma((2, PIECES)),
         ],
         compiler_params=pltpu.CompilerParams(
-            collective_id=0, has_side_effects=True, vmem_limit_bytes=67043328
+            collective_id=0, has_side_effects=True, vmem_limit_bytes=65400000
         ),
     )(query, grad_out, key_rows, value_rows)
-    parts = 4
     anywhere = pl.BlockSpec(memory_space=pl.ANY)
     return pl.pallas_call(
         finish,
@@ -491,15 +496,10 @@
             jax.ShapeDtypeStruct((tok, dh), F32),
             jax.ShapeDtypeStruct((tok, dh), F32),
         ),
-        in_specs=[anywhere] * 2,
+        in_specs=[pl.BlockSpec(memory_space=vmem)] * 2,
         out_specs=(anywhere,) * 3,
-        scratch_shapes=[
-            vmem((parts, tok // parts, heads * dh), BF16),
-            vmem((2, tok, dh), BF16),
-            vmem((2, tok, dh), F32),
-            dma((parts + 1,)),
-            dma((parts + 2,)),
-        ],
+        scratch_shapes=[vmem((2, tok, dh), F32), dma((3,))],
+        compiler_params=pltpu.CompilerParams(vmem_limit_bytes=8 << 20),
     )(grad_query, fin)
 
 

time: 56.4 us -> 53.6 us (0.950)
  Pallas kernels: 55.5 us -> 52.7 us
    pallas_call x1, Pallas kernels: 53 us -> 51.4 us  [on_device(): pl.pallas_call(kernel, out_shape=(vmem(query.shape, BF16), vmem((2, tok,...]
    pallas_call x1, Pallas kernels: 2.48 us -> 1.34 us  [on_device(): pl.pallas_call(finish, out_shape=(jax.ShapeDtypeStruct(query.shape, BF16)...]
where the time goes in v5:
time: 53.6 us; the launch traced here: 53.5 us
  Pallas kernels  52.7 us (98%)
  between operations  0.8 us (1%)
    pallas_call x1, Pallas kernels, on_device(): pl.pallas_call(kernel, out_shape=(vmem(query.shape, BF16), vmem((2, tok,...  51.4 us
    pallas_call x1, Pallas kernels, on_device(): pl.pallas_call(finish, out_shape=(jax.ShapeDtypeStruct(query.shape, BF16)...  1.34 us

profile of v5, /device:TPU:25, one launch (start us, length us, event | category | flops | bytes accessed | tf_op | source)
XLA Modules:
  0.0 53.5 jit_solution(7107799670204635275)
XLA Ops:
  0.6 51.4 %shard_map.67 = (bf16[512,1024]{1,0:T(8,128)(2,1)S(1)}, bf16[2,512,256]{2,1,0:T(8,128)(2,1)S(1)}) custom-call(bf16[512,1024]{1,0:T(8,128)(2,1)} %q_hbm.1, bf16[512,1024]{1,0:T(8,128)(2,1)} %g_hbm.1, bf16[512,256]{1,0:T(8,128)(2,1)} %k_hbm.1, bf16[512,256]{1,0:T(8,128)(2,1)} %v_hbm.1), custom_call_target="tpu_custom_call" | custom-call | tf_op jit(solution)/shard_map/pallas_call | solution.py:449
  52.0 1.3 %shard_map.68 = (bf16[512,1024]{1,0:T(8,128)(2,1)}, f32[512,256]{1,0:T(8,128)}, f32[512,256]{1,0:T(8,128)}) custom-call(bf16[512,1024]{1,0:T(8,128)(2,1)S(1)} %get-tuple-element.5.dq_in, bf16[2,512,256]{2,1,0:T(8,128)(2,1)S(1)} %get-tuple-element.6.fin_in), custom_call_target="tpu_custom_call" | custom-call | tf_op jit(solution)/shard_map/pallas_call | solution.py:492
